TPU v7x, 512 devices: a whole 4x8x8 slice. The times are simulated.
512 devices in a mesh: wide: 64 (over z, x, core), narrow: 8 (over y).
Axes of the slice: x: 4, y: 8, z: 8, core: 2. Of those that a mesh axis runs over, the one named last changes fastest.
Arguments:
- charges: float32 [64, 1048576], P(None, ('wide', 'narrow')), may hold values from -6 to 6
- leaf_angle: float32 [64, 65536], P(None, ('wide', 'narrow')), may hold values from -3.140625 to 3.140625
- lagrange: float32 [48, 64], replicated, may hold values from -0.75 to 0.75
- level_angle: float32 [2, 48, 65536], P(None, None, ('wide', 'narrow')), may hold values from -3.140625 to 3.140625
- level_self: float32 [2, 96, 96], replicated, may hold values from -0.4375 to 0.4375
- level_peer: float32 [2, 96, 96], replicated, may hold values from -0.4375 to 0.4375
- switch_angle: float32 [48, 65536], P(None, ('wide', 'narrow')), may hold values from -3.140625 to 3.140625
- switch_matrix: float32 [96, 96], replicated, may hold values from -0.625 to 0.625
- out_angle: float32 [64, 65536], P(None, ('wide', 'narrow')), may hold values from -3.140625 to 3.140625
- evaluate: float32 [64, 48], replicated, may hold values from -0.875 to 0.875
Outputs:
- field: bfloat16 [64, 1048576], P(None, ('wide', 'narrow'))
All inputs are finite; a program needn't handle non-finite values.
Results may differ from a plain program's by a relative error of at most 0.0049.
Values may be sent and summed in bfloat16 or wider, within the bound.
No kernel may reach another device: no remote copies, remote signals or barrier semaphores. Data moves between devices by JAX's collectives and lax.ppermute only.
A program may use at most 64 MiB of HBM per device.

v0:
```python
import jax
import jax.numpy as jnp
from jax import lax
from jax.sharding import PartitionSpec as P


def from_partner(value, axis, apart):
    mask = 2**apart
    pairs = [(source, source ^ mask) for source in range(lax.axis_size(axis))]
    return lax.ppermute(value, axis, pairs)


def product(left, right):
    return jnp.dot(left, right, precision=lax.Precision.HIGHEST, preferred_element_type=jnp.float32)


def rotate(boxes_state, phase_angle, per_box):
    rank = phase_angle.shape[0]
    cos_part = jnp.repeat(jnp.cos(phase_angle), per_box, axis=1)
    sin_part = jnp.repeat(jnp.sin(phase_angle), per_box, axis=1)
    real_part = boxes_state[:rank]
    imag_part = boxes_state[rank:]
    return jnp.concatenate(
        [cos_part * real_part - sin_part * imag_part, sin_part * real_part + cos_part * imag_part],
        axis=0,
    )


def butterfly_level(boxes_state, self_matrix, peer_matrix, phase_angle, bit, per_box):
    sent_state = boxes_state.astype(jnp.bfloat16)
    received = from_partner(sent_state, "narrow", bit)
    combined = product(self_matrix, boxes_state) + product(
        peer_matrix, received.astype(jnp.float32)
    )
    return rotate(combined, phase_angle, per_box)


def leaf_weights(lagrange, point_charges, point_angle, per_box):
    cos_leaf = jnp.repeat(jnp.cos(point_angle), per_box, axis=1)
    sin_leaf = jnp.repeat(jnp.sin(point_angle), per_box, axis=1)
    return jnp.concatenate(
        [product(lagrange, cos_leaf * point_charges), product(lagrange, sin_leaf * point_charges)],
        axis=0,
    )


def body(
    charges,
    leaf_angle,
    lagrange,
    level_angle,
    level_self,
    level_peer,
    switch_angle,
    switch_matrix,
    out_angle,
    evaluate,
):
    per_box = charges.shape[1] // leaf_angle.shape[1]
    rank = lagrange.shape[0]
    last_bit = lax.axis_size("narrow").bit_length() - 2
    boxes_state = leaf_weights(lagrange, charges, leaf_angle, per_box)
    boxes_state = butterfly_level(
        boxes_state, level_self[0], level_peer[0], level_angle[0], 0, per_box
    )
    boxes_state = lax.all_to_all(boxes_state, "wide", split_axis=1, concat_axis=1, tiled=True)
    boxes_state = rotate(product(switch_matrix, boxes_state), switch_angle, per_box)
    boxes_state = butterfly_level(
        boxes_state, level_self[1], level_peer[1], level_angle[1], last_bit, per_box
    )
    real_part = product(evaluate, boxes_state[:rank])
    imag_part = product(evaluate, boxes_state[rank:])
    cos_out = jnp.repeat(jnp.cos(out_angle), per_box, axis=1)
    sin_out = jnp.repeat(jnp.sin(out_angle), per_box, axis=1)
    return (cos_out * real_part - sin_out * imag_part).astype(jnp.bfloat16)


def solution(mesh):
    return jax.shard_map(
        body,
        mesh=mesh,
        in_specs=(
            P(None, ("wide", "narrow")),
            P(None, ("wide", "narrow")),
            P(),
            P(None, None, ("wide", "narrow")),
            P(),
            P(),
            P(None, ("wide", "narrow")),
            P(),
            P(None, ("wide", "narrow")),
            P(),
        ),
        out_specs=P(None, ("wide", "narrow")),
        check_vma=False,
    )
```

profile of v0, /device:TPU:56, one launch (start us, length us, event | category | flops | bytes accessed | tf_op | source)
XLA Modules:
  0.0 94.1 jit_solution(16708297158461650053)
XLA Ops:
  0.0 0.9 fusion.31
  1.1 1.4 %copy.16 = f32[64,2048]{0,1:T(8,128)S(1)} copy(f32[64,2048]{1,0:T(8,128)} %param.10) | data formatting | bytes 1048576 | tf_op args[0]
  2.6 0.6 copy-done.9
  3.2 1.3 %convolution_bitcast_fusion.3 = f32[48,2048]{1,0:T(8,128)S(1)} fusion(f32[64,2048]{0,1:T(8,128)S(1)} %get-tuple-element.10, f32[48,64]{1,0:T(8,128)S(1)} %copy-done.9), kind=kOutput, calls=%fused_computation.11 | convolution fusion | flops 75497472 | bytes 929792 | tf_op jit(solution)/shard_map/dot_general | solution.py:14
  4.5 1.3 %convolution_bitcast_fusion.4 = f32[48,2048]{1,0:T(8,128)S(1)} fusion(f32[64,2048]{0,1:T(8,128)S(1)} %get-tuple-element.9, f32[48,64]{1,0:T(8,128)S(1)} %copy-done.9), kind=kOutput, calls=%fused_computation.12 | convolution fusion | flops 75497472 | bytes 929792 | tf_op jit(solution)/shard_map/dot_general | solution.py:14
  5.8 3.3 %collective-permute-start = (bf16[96,2048]{1,0:T(8,128)(2,1)S(1)}, bf16[96,2048]{1,0:T(8,128)(2,1)S(1)}, u32[]{:S(2)}, u32[]{:S(2)}) collective-permute-start(bf16[96,2048]{1,0:T(8,128)(2,1)S(1)} %fusion.8), channel_id=1, source_target_pairs={{0,1},{1,0},{2,3},{3,2},{4,5},{5,4},{6,7},{7,6},{8,9},{9,8},{10,11... | collective-permute-start | bytes 1179656 | tf_op jit(solution)/shard_map/ppermute | solution.py:10
  9.1 0.8 sine_bitcast_fusion.1
  10.9 0.6 copy-done.4
  11.5 0.8 fusion.9
  12.3 6.3 %collective-permute-done = bf16[96,2048]{1,0:T(8,128)(2,1)S(1)} collective-permute-done((bf16[96,2048]{1,0:T(8,128)(2,1)S(1)}, bf16[96,2048]{1,0:T(8,128)(2,1)S(1)}, u32[]{:S(2)}, u32[]{:S(2)}) %collective-permute-start) | collective-permute-done | bytes 393248 | tf_op jit(solution)/shard_map/ppermute | solution.py:10
  18.6 0.5 fusion.1
  19.2 1.3 %copy.24 = f32[96,2048]{0,1:T(8,128)} copy(f32[96,2048]{1,0:T(8,128)S(1)} %pad_maximum_fusion.1) | data formatting | bytes 1572864 | tf_op jit(solution)/shard_map/concatenate | solution.py:23
  20.5 13.9 %all-to-all-start = ((f32[96,64,32]{0,2,1:T(8,128)}), f32[96,64,32]{0,2,1:T(8,128)S(1)}, u32[]{:S(2)}, u32[]{:S(2)}) async-start(f32[96,64,32]{0,2,1:T(8,128)} %bitcast.15), calls=%async_computation | async-start | bytes 2097152 | tf_op jit(solution)/shard_map/all_to_all | solution.py:66
  35.3 1.1 %copy.27 = f32[48,2048]{1,0:T(8,128)} copy(f32[48,2048]{0,1:T(8,128)S(1)} %bitcast.70) | data formatting | bytes 786432 | tf_op jit(solution)/shard_map/reshape | solution.py:20
  37.7 25.6 %all-to-all-done = f32[96,64,32]{0,2,1:T(8,128)S(1)} async-done(((f32[96,64,32]{0,2,1:T(8,128)}), f32[96,64,32]{0,2,1:T(8,128)S(1)}, u32[]{:S(2)}, u32[]{:S(2)}) %all-to-all-start) | async-done | bytes 786464 | tf_op jit(solution)/shard_map/all_to_all | solution.py:66
  63.4 1.2 %convolution_bitcast_fusion = f32[96,2048]{1,0:T(8,128)S(1)} fusion(f32[96,2048]{0,1:T(8,128)S(1)} %bitcast.66, f32[96,96]{1,0:T(8,128)S(1)} %copy-done), kind=kOutput, calls=%fused_computation | convolution fusion | flops 226492416 | bytes 1609728 | tf_op jit(solution)/shard_map/dot_general | solution.py:14
  64.7 0.8 fusion.6
  65.5 4.9 %collective-permute-start.1 = (bf16[96,2048]{1,0:T(8,128)(2,1)}, bf16[96,2048]{1,0:T(8,128)(2,1)}, u32[]{:S(2)}, u32[]{:S(2)}) collective-permute-start(bf16[96,2048]{1,0:T(8,128)(2,1)} %fusion.6), channel_id=1, source_target_pairs={{0,4},{1,5},{2,6},{3,7},{4,0},{5,1},{6,2},{7,3},{8,12},{9,13},{10,... | collective-permute-start | bytes 1179656 | tf_op jit(solution)/shard_map/ppermute | solution.py:10
  71.2 1.1 %copy.37 = f32[64,2048]{1,0:T(8,128)} copy(f32[64,2048]{0,1:T(8,128)S(1)} %bitcast.74) | data formatting | bytes 1048576 | tf_op jit(solution)/shard_map/reshape | solution.py:74
  72.3 0.8 fusion.7
  73.2 17.1 %collective-permute-done.1 = bf16[96,2048]{1,0:T(8,128)(2,1)} collective-permute-done((bf16[96,2048]{1,0:T(8,128)(2,1)}, bf16[96,2048]{1,0:T(8,128)(2,1)}, u32[]{:S(2)}, u32[]{:S(2)}) %collective-permute-start.1) | collective-permute-done | bytes 393248 | tf_op jit(solution)/shard_map/ppermute | solution.py:10
  90.3 1.5 %fusion = f32[96,2048]{1,0:T(8,128)S(1)} fusion(f32[2048,96]{0,1:T(8,128)S(1)} %fusion.7, bf16[96,2048]{1,0:T(8,128)(2,1)} %collective-permute-done.1, f32[2,96,96]{2,1,0:T(8,128)S(1)} %copy-done.8), kind=kOutput, calls=%fused_computation.2 | convolution fusion | flops 226689024 | bytes 2015232 | tf_op jit(solution)/shard_map/dot_general | solution.py:14
  91.8 0.6 fusion.4
  92.8 1.3 %fusion.5 = bf16[64,2048]{1,0:T(8,128)(2,1)} fusion(f32[64,2048]{1,0:T(8,128)S(1)} %fusion.4, f32[64,2048]{1,0:T(8,128)S(1)} %copy-done.1, f32[64,48]{0,1:T(8,128)S(1)} %copy-done.3, f32[48,2048]{1,0:T(8,128)S(1)} %copy.30, f32[48,2048]{1,0:T(8,128)S(1)} %copy.32, f32[96,2048]{1,0:T(8,128)S(1)} %fusion), kind=kOutput, calls=%fused_computation.10 | convolution fusion | flops 76185600 | bytes 2895872 | tf_op jit(solution)/shard_map/dot_general | solution.py:14
  (55 shorter events, 4.9 us)
Async XLA Ops:
  0.0 63.4 %copy-start = (f32[96,96]{1,0:T(8,128)S(1)}, f32[96,96]{1,0:T(8,128)}, u32[]{:S(2)}) copy-start(f32[96,96]{1,0:T(8,128)} %param.17) | copy-start | bytes 110596
  2.5 0.7 copy-start.9
  5.8 3.3 %copy-start.10 = (f32[2,48,128]{2,1,0:T(8,128)S(1)}, f32[2,48,128]{2,1,0:T(8,128)}, u32[]{:S(2)}) copy-start(f32[2,48,128]{2,1,0:T(8,128)} %param.13) | copy-start | bytes 147460
  5.8 12.8 %collective-permute-start = (bf16[96,2048]{1,0:T(8,128)(2,1)S(1)}, bf16[96,2048]{1,0:T(8,128)(2,1)S(1)}, u32[]{:S(2)}, u32[]{:S(2)}) collective-permute-start(bf16[96,2048]{1,0:T(8,128)(2,1)S(1)} %fusion.8), channel_id=1, source_target_pairs={{0,1},{1,0},{2,3},{3,2},{4,5},{5,4},{6,7},{7,6},{8,9},{9,8},{10,11... | collective-permute-start | bytes 1179656 | tf_op jit(solution)/shard_map/ppermute | solution.py:10
  10.6 0.9 copy-start.4
  11.5 7.1 %copy-start.7 = (f32[2,96,96]{2,1,0:T(8,128)S(1)}, f32[2,96,96]{2,1,0:T(8,128)}, u32[]{:S(2)}) copy-start(f32[2,96,96]{2,1,0:T(8,128)} %param.15) | copy-start | bytes 221188
  20.5 13.9 %copy-start.12 = (f32[48,128]{1,0:T(8,128)S(1)}, f32[48,128]{1,0:T(8,128)}, u32[]{:S(2)}) copy-start(f32[48,128]{1,0:T(8,128)} %param.16) | copy-start | bytes 73732
  20.5 42.8 %all-to-all-start = ((f32[96,64,32]{0,2,1:T(8,128)}), f32[96,64,32]{0,2,1:T(8,128)S(1)}, u32[]{:S(2)}, u32[]{:S(2)}) async-start(f32[96,64,32]{0,2,1:T(8,128)} %bitcast.15), calls=%async_computation | async-start | bytes 2097152 | tf_op jit(solution)/shard_map/all_to_all | solution.py:66
  35.3 1.1 %copy-start.6 = (f32[48,128]{1,0:T(8,128)S(1)}, f32[48,128]{1,0:T(8,128)}, u32[]{:S(2)}) copy-start(f32[48,128]{1,0:T(8,128)} %get-tuple-element.14) | copy-start | bytes 73732
  36.5 0.7 copy-start.5
  63.4 1.2 %copy-start.2 = (f32[48,2048]{1,0:T(8,128)S(1)}, f32[48,2048]{1,0:T(8,128)}, u32[]{:S(2)}) copy-start(f32[48,2048]{1,0:T(8,128)} %copy.27) | copy-start | bytes 1179652
  64.7 5.7 %copy-start.11 = (f32[64,128]{1,0:T(8,128)S(1)}, f32[64,128]{1,0:T(8,128)}, u32[]{:S(2)}) copy-start(f32[64,128]{1,0:T(8,128)} %param.18) | copy-start | bytes 98308
  65.5 24.8 %collective-permute-start.1 = (bf16[96,2048]{1,0:T(8,128)(2,1)}, bf16[96,2048]{1,0:T(8,128)(2,1)}, u32[]{:S(2)}, u32[]{:S(2)}) collective-permute-start(bf16[96,2048]{1,0:T(8,128)(2,1)} %fusion.6), channel_id=1, source_target_pairs={{0,4},{1,5},{2,6},{3,7},{4,0},{5,1},{6,2},{7,3},{8,12},{9,13},{10,... | collective-permute-start | bytes 1179656 | tf_op jit(solution)/shard_map/ppermute | solution.py:10
  72.3 17.9 %copy-start.8 = (f32[2,96,96]{2,1,0:T(8,128)S(1)}, f32[2,96,96]{2,1,0:T(8,128)}, u32[]{:S(2)}) copy-start(f32[2,96,96]{2,1,0:T(8,128)} %param.15) | copy-start | bytes 221188
  73.2 18.6 %copy-start.3 = (f32[64,48]{0,1:T(8,128)S(1)}, f32[64,48]{0,1:T(8,128)}, u32[]{:S(2)}) copy-start(f32[64,48]{0,1:T(8,128)} %param.19) | copy-start | bytes 36868
  91.8 1.0 %copy-start.1 = (f32[64,2048]{1,0:T(8,128)S(1)}, f32[64,2048]{1,0:T(8,128)}, u32[]{:S(2)}) copy-start(f32[64,2048]{1,0:T(8,128)} %copy.37) | copy-start | bytes 1572868
where the time goes:
time: 94.9 us; the launch traced here: 94.1 us
  waiting for transfers between devices  49 us (52%)
  starting transfers between devices  22.1 us (23%)
  local copies, waits for them, and re-layouts  12.2 us (13%)
  matrix products  9.29 us (10%)
  other arithmetic  1.23 us (1%)
    all_to_all x1, waiting for transfers between devices, body(): lax.all_to_all(boxes_state, 'wide', split_axis=1, concat_axis=1, tiled=True)  25.6 us
    ppermute x2, waiting for transfers between devices, from_partner(): return lax.ppermute(value, axis, pairs)  23.3 us
    all_to_all x1, starting transfers between devices, body(): lax.all_to_all(boxes_state, 'wide', split_axis=1, concat_axis=1, tiled=True)  13.9 us
    dot_general x9, matrix products, product(): jnp.dot(left, right, precision=lax.Precision.HIGHEST, preferred_element_t...  9.29 us
    ppermute x2, starting transfers between devices, from_partner(): return lax.ppermute(value, axis, pairs)  8.14 us
    unnamed x27, local copies, waits for them, and re-layouts  3.41 us
  transfers between devices with their start and end apart: 3, of which 3 were waited for; matrix products, arithmetic and copies ran while one was open for 9% of the time, Pallas kernels for 0%

commit v1 on v0

v1 whole, which is shorter than its diff:
```python
import jax
import jax.numpy as jnp
from jax import lax
from jax.experimental import pallas as pl
from jax.experimental.pallas import tpu as pltpu
from jax.sharding import PartitionSpec as P

F32 = jnp.float32
BF16 = jnp.bfloat16
LANES = 128
CHUNK = 256


def sin_cos(angle):
    turns = jnp.floor(angle * 0.6366197723675814 + 0.5)
    rest = angle - turns * 1.5703125
    rest = rest - turns * 4.837512969970703125e-4
    rest = rest - turns * 7.549789948768648e-8
    square = rest * rest
    sine = rest + rest * square * (
        -1.6666654611e-1 + square * (8.3321608736e-3 + square * -1.9515295891e-4)
    )
    cosine = (
        1.0
        - 0.5 * square
        + square
        * square
        * (4.166664568298827e-2 + square * (-1.388731625493765e-3 + square * 2.443315711809948e-5))
    )
    size = jnp.abs(turns)
    odd = size == 1.0
    sign = jnp.where(size == 2.0, -1.0, 1.0)
    return (
        jnp.where(odd, turns * cosine, sign * sine),
        jnp.where(odd, -turns * sine, sign * cosine),
    )


def halves(value):
    high = value.astype(BF16)
    return high, (value - high.astype(F32)).astype(BF16)


def dot(left, right):
    return jnp.dot(left, right, preferred_element_type=F32)


def dot_full(left, right, dims=((1,), (0,))):
    return lax.dot_general(
        left, right, (dims, ((), ())), precision=lax.Precision.HIGHEST, preferred_element_type=F32
    )


def spread(rows, scratch):
    scratch[...] = jnp.zeros((LANES, LANES), F32)
    for to_row, from_row in ((0, 0), (64, 48)):
        for to_lane, from_lane in ((0, 0), (64, 48)):
            scratch[to_row : to_row + 48, to_lane : to_lane + 48] = rows[
                from_row : from_row + 48, from_lane : from_lane + 48
            ]
    return scratch[...]


def two_blocks(block, scratch):
    scratch[...] = jnp.zeros((LANES, LANES), F32)
    scratch[0:48, 0:64] = block
    scratch[64:112, 64:128] = block
    return scratch[...]


def rotation_factors(angle):
    sine, cosine = sin_cos(angle)
    gap = jnp.zeros((16, LANES), F32)
    cos_rows = jnp.concatenate([cosine, gap, cosine, gap], axis=0)
    sin_rows = jnp.concatenate([-sine, gap, sine, gap], axis=0)
    return cos_rows.T, sin_rows.T


def per_box(value, factor):
    boxes = factor.shape[0]
    return (value.reshape(boxes, 16, LANES) * factor[:, None, :]).reshape(boxes * 16, LANES)


def rotated(value, cos_factor, sin_factor):
    return per_box(value, cos_factor) + per_box(pltpu.roll(value, 64, 1), sin_factor)


def pack_kernel(charges, leaf_angle, out):
    for tile in range(16):
        out[tile] = charges[:, tile * LANES : (tile + 1) * LANES].astype(BF16)
    high, low = halves(leaf_angle[...])
    out[16] = high
    out[17] = low


def source_part(read_tile, factors, weights_high, weights_low, emit):
    for chunk in range(2048 // CHUNK):
        rows = []
        for tile in range(chunk * CHUNK // LANES, (chunk + 1) * CHUNK // LANES):
            points = read_tile(tile)
            rows.append(jnp.concatenate([points, points], axis=0).T)
        value = jnp.concatenate(rows, axis=0)
        boxes = CHUNK // 16
        value = per_box(value, factors[chunk * boxes : (chunk + 1) * boxes, :])
        high, low = halves(value)
        emit(chunk, dot(high, weights_high) + dot(low, weights_high) + dot(high, weights_low))


def own_kernel(
    charges, leaf_angle, lagrange, level_angle, level_self, level_peer, own, weights, factors, scratch, turned
):
    leaf = two_blocks(lagrange[...], scratch)
    self_matrix = spread(level_self.at[0], scratch)
    own_weights = dot_full(leaf, self_matrix, ((0,), (1,)))
    peer_matrix = spread(level_peer.at[0], scratch)
    peer_weights = dot_full(leaf, peer_matrix, ((0,), (1,)))
    weights[0], weights[1] = halves(peer_weights)
    factors[0], factors[1] = rotation_factors(level_angle[0])
    sine, cosine = sin_cos(leaf_angle[...])
    turned[...] = jnp.concatenate([cosine, sine], axis=0).T
    own_high, own_low = halves(own_weights)

    def emit(chunk, value):
        own[chunk * CHUNK : (chunk + 1) * CHUNK, :] = value

    source_part(
        lambda tile: charges[:, tile * LANES : (tile + 1) * LANES], turned, own_high, own_low, emit
    )


def peer_kernel(received, own, weights, factors, out, turned):
    sine, cosine = sin_cos(received[16].astype(F32) + received[17].astype(F32))
    turned[...] = jnp.concatenate([cosine, sine], axis=0).T
    lane = lax.broadcasted_iota(jnp.int32, (CHUNK // 4, LANES), 1) % 64
    boxes = CHUNK // 16

    def emit(chunk, value):
        value = value + own[chunk * CHUNK : (chunk + 1) * CHUNK, :]
        value = rotated(
            value,
            factors[0, chunk * boxes : (chunk + 1) * boxes, :],
            factors[1, chunk * boxes : (chunk + 1) * boxes, :],
        )
        parts = value.reshape(CHUNK // 32, 4, 8, LANES)
        last = parts[:, 3].reshape(CHUNK // 4, LANES)
        packed = [
            jnp.where(lane < 48, parts[:, i].reshape(CHUNK // 4, LANES), pltpu.roll(last, shift, 1)).reshape(
                CHUNK // 32, 1, 8, LANES
            )
            for i, shift in enumerate((48, 32, 16))
        ]
        packed = jnp.concatenate(packed, axis=1).reshape(CHUNK * 3 // 4, LANES)
        out[chunk * CHUNK * 3 // 4 : (chunk + 1) * CHUNK * 3 // 4, :] = packed.astype(BF16)

    source_part(lambda tile: received[tile].astype(F32), turned, weights[0], weights[1], emit)


def target_kernel(
    level_angle, peer_angle, switch_angle, out_angle, level_self, level_peer, switch_matrix, evaluate, weights, factors, scratch
):
    weights[0], weights[1] = halves(spread(switch_matrix, scratch).T)
    weights[2], weights[3] = halves(spread(level_peer.at[1], scratch).T)
    weights[4], weights[5] = halves(spread(level_self.at[1], scratch).T)
    scratch[...] = jnp.zeros((LANES, LANES), F32)
    scratch[0:64, 0:48] = evaluate[...]
    scratch[64:128, 64:112] = evaluate[...]
    weights[6], weights[7] = halves(scratch[...].T)
    factors[0], factors[1] = rotation_factors(switch_angle[...])
    factors[2], factors[3] = rotation_factors(level_angle[1])
    sine, cosine = sin_cos(out_angle[...])
    factors[4] = jnp.concatenate([cosine, -sine], axis=0).T
    factors[5], factors[6] = rotation_factors(peer_angle[0:48])
    sine, cosine = sin_cos(peer_angle[48:112])
    factors[7] = jnp.concatenate([cosine, -sine], axis=0).T


def evaluated(value, cos_factor, sin_factor, out_factor, weights):
    value = rotated(value, cos_factor, sin_factor)
    high, low = halves(value)
    value = dot(high, weights[6]) + dot(low, weights[6]) + dot(high, weights[7])
    value = per_box(value, out_factor)
    tiles = []
    for tile in range(CHUNK // LANES):
        turned = value[tile * LANES : (tile + 1) * LANES, :].T
        tiles.append(turned[0:64] + turned[64:128])
    return jnp.concatenate(tiles, axis=1)


def switch_kernel(received, weights, factors, middle, sent):
    lane = lax.broadcasted_iota(jnp.int32, (CHUNK // 4, LANES), 1) % 64
    boxes = CHUNK // 16
    for chunk in range(2048 // CHUNK):
        packed = received[chunk * CHUNK * 3 // 4 : (chunk + 1) * CHUNK * 3 // 4, :].astype(F32)
        parts = packed.reshape(CHUNK // 32, 3, 8, LANES)
        first = [parts[:, i].reshape(CHUNK // 4, LANES) for i in range(3)]
        last = jnp.where(
            lane < 16,
            pltpu.roll(first[0], 80, 1),
            jnp.where(lane < 32, pltpu.roll(first[1], 96, 1), pltpu.roll(first[2], 112, 1)),
        )
        value = jnp.concatenate(
            [part.reshape(CHUNK // 32, 1, 8, LANES) for part in first + [last]], axis=1
        ).reshape(CHUNK, LANES)
        value = value.astype(BF16)
        value = dot(value, weights[0]) + dot(value, weights[1])
        here = pl.ds(chunk * boxes, boxes)
        value = rotated(value, factors[0, here, :], factors[1, here, :])
        middle[chunk * CHUNK : (chunk + 1) * CHUNK, :] = value
        value = value.astype(BF16)
        value = dot(value, weights[2]) + dot(value, weights[3])
        value = evaluated(value, factors[5, here, :], factors[6, here, :], factors[7, here, :], weights)
        sent[:, chunk * CHUNK : (chunk + 1) * CHUNK] = value.astype(BF16)


def last_kernel(middle, weights, factors, own):
    boxes = CHUNK // 16
    for chunk in range(2048 // CHUNK):
        high, low = halves(middle[chunk * CHUNK : (chunk + 1) * CHUNK, :])
        value = dot(high, weights[4]) + dot(low, weights[4]) + dot(high, weights[5])
        here = pl.ds(chunk * boxes, boxes)
        own[:, chunk * CHUNK : (chunk + 1) * CHUNK] = evaluated(
            value, factors[2, here, :], factors[3, here, :], factors[4, here, :], weights
        )


def add_kernel(own, received, out):
    out[...] = (own[...] + received[...].astype(F32)).astype(BF16)


def call(kernel, outs, args, scratch=(), name=None):
    whole = pl.BlockSpec(memory_space=pltpu.VMEM)
    shapes = [jax.ShapeDtypeStruct(shape, dtype) for shape, dtype in outs]
    return pl.pallas_call(
        kernel,
        out_shape=shapes if len(shapes) > 1 else shapes[0],
        in_specs=[whole] * len(args),
        out_specs=[whole] * len(shapes) if len(shapes) > 1 else whole,
        scratch_shapes=[pltpu.VMEM((LANES, LANES), F32)] * scratch if scratch else [],
        compiler_params=pltpu.CompilerParams(vmem_limit_bytes=32 * 1024 * 1024),
        name=name,
    )(*args)


def from_partner(value, apart):
    pairs = [(source, source ^ apart) for source in range(lax.axis_size("narrow"))]
    return lax.ppermute(value, "narrow", pairs)


def body(
    charges,
    leaf_angle,
    lagrange,
    level_angle,
    level_self,
    level_peer,
    switch_angle,
    switch_matrix,
    out_angle,
    evaluate,
):
    square = (LANES, LANES)
    packed = call(pack_kernel, [((18, 64, LANES), BF16)], [charges, leaf_angle], name="pack")
    near = from_partner(packed, 1)
    far_angle = from_partner(jnp.concatenate([level_angle[1], out_angle], axis=0), 4)
    own, weights, factors = call(
        own_kernel,
        [((2048, LANES), F32), ((2, *square), BF16), ((2, *square), F32)],
        [charges, leaf_angle, lagrange, level_angle, level_self, level_peer],
        2,
        name="own",
    )
    state = call(peer_kernel, [((1536, LANES), BF16)], [near, own, weights, factors], 1, name="peer")
    state = lax.all_to_all(state.reshape(64, 24, LANES), "wide", 0, 0, tiled=True).reshape(1536, LANES)
    weights, factors = call(
        target_kernel,
        [((8, *square), BF16), ((8, *square), F32)],
        [level_angle, far_angle, switch_angle, out_angle, level_self, level_peer, switch_matrix, evaluate],
        1,
        name="target",
    )
    middle, sent = call(
        switch_kernel,
        [((2048, LANES), F32), ((64, 2048), BF16)],
        [state, weights, factors],
        name="switch",
    )
    far = from_partner(sent, 4)
    own = call(last_kernel, [((64, 2048), F32)], [middle, weights, factors], name="last")
    return call(add_kernel, [((64, 2048), BF16)], [own, far], name="add")


def solution(mesh):
    return jax.shard_map(
        body,
        mesh=mesh,
        in_specs=(
            P(None, ("wide", "narrow")),
            P(None, ("wide", "narrow")),
            P(),
            P(None, None, ("wide", "narrow")),
            P(),
            P(),
            P(None, ("wide", "narrow")),
            P(),
            P(None, ("wide", "narrow")),
            P(),
        ),
        out_specs=P(None, ("wide", "narrow")),
        check_vma=False,
    )
```

time: 94.9 us -> 67.4 us (0.71)
  waiting for transfers between devices: 49 us -> 28.9 us
  local copies, waits for them, and re-layouts: 12.2 us -> 2.65 us
  matrix products: 9.29 us -> 0 us
  Pallas kernels: 0 us -> 8.41 us
  starting transfers between devices: 22.1 us -> 26.7 us
  other arithmetic: 1.23 us -> 0.01 us
    all_to_all x1, waiting for transfers between devices: 25.6 us -> 2.66 us  [body(): lax.all_to_all(state.reshape(64, 24, LANES), 'wide', 0, 0, tiled=True)]
    dot_general x9 -> x0, matrix products: 9.29 us -> none  [product(): jnp.dot(left, right, precision=lax.Precision.HIGHEST, preferred_element_t...]
    pallas_call x0 -> x7, Pallas kernels: none -> 8.41 us  [call(): pl.pallas_call(kernel, out_shape=shapes if len(shapes) > 1 else shapes[0]...]
    ppermute x2 -> x3, starting transfers between devices: 8.14 us -> 12.9 us  [from_partner(): return lax.ppermute(value, 'narrow', pairs)]
    reshape x8 -> x0, local copies, waits for them, and re-layouts: 4.06 us -> none  [the longest x3 1.7 us: rotate(): sin_part = jnp.repeat(jnp.sin(phase_angle), per_box, axis=1)]
    ppermute x2 -> x3, waiting for transfers between devices: 23.3 us -> 26.2 us  [from_partner(): return lax.ppermute(value, 'narrow', pairs)]
    sin x8 -> x0, local copies, waits for them, and re-layouts: 1.49 us -> none  [the longest x5 1.18 us: rotate(): sin_part = jnp.repeat(jnp.sin(phase_angle), per_box, axis=1)]
    cos x6 -> x0, local copies, waits for them, and re-layouts: 1.36 us -> none  [the longest x2 0.99 us: leaf_weights(): cos_leaf = jnp.repeat(jnp.cos(point_angle), per_box, axis=1)]
  transfers between devices with their start and end apart: 3 -> 4, of which waited for: 3 -> 4; matrix products, arithmetic and copies ran while one was open for 9% -> 0% of each run, Pallas kernels for 0% -> 4%
where the time goes in v1:
time: 67.4 us; the launch traced here: 66.8 us
  waiting for transfers between devices  28.9 us (43%)
  starting transfers between devices  26.7 us (40%)
  Pallas kernels  8.41 us (12%)
  local copies, waits for them, and re-layouts  2.65 us (4%)
    ppermute x3, waiting for transfers between devices, from_partner(): return lax.ppermute(value, 'narrow', pairs)  26.2 us
    all_to_all x1, starting transfers between devices, body(): lax.all_to_all(state.reshape(64, 24, LANES), 'wide', 0, 0, tiled=True)  13.8 us
    ppermute x3, starting transfers between devices, from_partner(): return lax.ppermute(value, 'narrow', pairs)  12.9 us
    pallas_call x7, Pallas kernels, call(): pl.pallas_call(kernel, out_shape=shapes if len(shapes) > 1 else shapes[0]...  8.41 us
    all_to_all x1, waiting for transfers between devices, body(): lax.all_to_all(state.reshape(64, 24, LANES), 'wide', 0, 0, tiled=True)  2.66 us
    unnamed x21, local copies, waits for them, and re-layouts  2.65 us
  transfers between devices with their start and end apart: 4, of which 4 were waited for; matrix products, arithmetic and copies ran while one was open for 0% of the time, Pallas kernels for 4%

profile of v1, /device:TPU:56, one launch (start us, length us, event | category | flops | bytes accessed | tf_op | source)
XLA Modules:
  0.0 66.8 jit_solution(11945005258276660694)
XLA Ops:
  0.0 1.0 %copy-done = f32[64,2048]{1,0:T(8,128)S(1)} copy-done((f32[64,2048]{1,0:T(8,128)S(1)}, f32[64,2048]{1,0:T(8,128)}, u32[]{:S(2)}) %copy-start) | copy-done | bytes 524312
  1.0 0.8 %copy-done.5 = f32[64,128]{1,0:T(8,128)S(1)} copy-done((f32[64,128]{1,0:T(8,128)S(1)}, f32[64,128]{1,0:T(8,128)}, u32[]{:S(2)}) %copy-start.5) | copy-done | bytes 32792
  1.9 3.4 %collective-permute-start = (bf16[18,64,128]{2,1,0:T(8,128)(2,1)S(1)}, bf16[18,64,128]{2,1,0:T(8,128)(2,1)S(1)}, u32[]{:S(2)}, u32[]{:S(2)}) collective-permute-start(bf16[18,64,128]{2,1,0:T(8,128)(2,1)S(1)} %pack.1), channel_id=1, source_target_pairs={{0,1},{1,0},{2,3},{3,2},{4,5},{5,4},{6,7},{7,6},{8,9},{9,8},{10,11... | collective-permute-start | bytes 884744 | tf_op jit(solution)/shard_map/ppermute | solution.py:246
  5.3 0.0 copy-done.1
  5.3 0.0 copy-done.2
  5.3 0.0 copy-done.3
  5.3 0.0 copy-done.7
  5.3 1.1 %own.1 = (f32[2048,128]{1,0:T(8,128)S(1)}, bf16[2,128,128]{2,1,0:T(8,128)(2,1)S(1)}, f32[2,128,128]{2,1,0:T(8,128)S(1)}) custom-call(f32[64,2048]{1,0:T(8,128)S(1)} %copy-done, f32[64,128]{1,0:T(8,128)S(1)} %copy-done.5, f32[48,64]{1,0:T(8,128)S(1)} %copy-done.7, f32[2,48,128]{2,1,0:T(8,128)S(1)} %copy-done.3, f32[2,96,96]{2,1,0:T(8,128)S(1)} %copy-done.1, ...), custom_call_target="tpu_custom_call" | custom-call | tf_op jit(solution)/shard_map/own/pallas_call | solution.py:233
  6.4 6.3 %collective-permute-done.received = bf16[18,64,128]{2,1,0:T(8,128)(2,1)S(1)} collective-permute-done((bf16[18,64,128]{2,1,0:T(8,128)(2,1)S(1)}, bf16[18,64,128]{2,1,0:T(8,128)(2,1)S(1)}, u32[]{:S(2)}, u32[]{:S(2)}) %collective-permute-start) | collective-permute-done | bytes 294944 | tf_op jit(solution)/shard_map/ppermute | solution.py:246
  12.6 1.8 %peer.1 = bf16[1536,128]{1,0:T(8,128)(2,1)} custom-call(bf16[18,64,128]{2,1,0:T(8,128)(2,1)S(1)} %collective-permute-done.received, f32[2048,128]{1,0:T(8,128)S(1)} %get-tuple-element.12.own, bf16[2,128,128]{2,1,0:T(8,128)(2,1)S(1)} %get-tuple-element.13.weights, f32[2,128,128]{2,1,0:T(8,128)S(1)} %get-tuple-element.14.factors), custom_call_target="tpu_custom_call" | custom-call | tf_op jit(solution)/shard_map/peer/pallas_call | solution.py:233
  14.4 13.8 %all-to-all-start = ((bf16[64,24,128]{2,1,0:T(8,128)(2,1)}), bf16[64,24,128]{2,1,0:T(8,128)(2,1)S(1)}, u32[]{:S(2)}, u32[]{:S(2)}) async-start(bf16[64,24,128]{2,1,0:T(8,128)(2,1)} %bitcast), calls=%async_computation | async-start | bytes 786432 | tf_op jit(solution)/shard_map/all_to_all | solution.py:273
  28.2 0.0 copy-start.4
  28.2 0.7 %copy-done.4 = f32[64,128]{1,0:T(8,128)S(1)} copy-done((f32[64,128]{1,0:T(8,128)S(1)}, f32[64,128]{1,0:T(8,128)}, u32[]{:S(2)}) %copy-start.4) | copy-done | bytes 32792
  29.0 0.0 copy-start.6
  29.0 4.8 %collective-permute-start.1 = (f32[112,128]{1,0:T(8,128)S(1)}, f32[112,128]{1,0:T(8,128)S(1)}, u32[]{:S(2)}, u32[]{:S(2)}) collective-permute-start(f32[112,128]{1,0:T(8,128)S(1)} %pad_maximum_fusion), channel_id=1, source_target_pairs={{0,4},{1,5},{2,6},{3,7},{4,0},{5,1},{6,2},{7,3},{8,12},{9,13},{10,... | collective-permute-start | bytes 172040 | tf_op jit(solution)/shard_map/ppermute | solution.py:246
  33.9 0.1 copy.11.evaluate
  33.9 6.1 %collective-permute-done.1.peer_angle = f32[112,128]{1,0:T(8,128)S(1)} collective-permute-done((f32[112,128]{1,0:T(8,128)S(1)}, f32[112,128]{1,0:T(8,128)S(1)}, u32[]{:S(2)}, u32[]{:S(2)}) %collective-permute-start.1) | collective-permute-done | bytes 57376 | tf_op jit(solution)/shard_map/ppermute | solution.py:246
  40.0 0.4 target.1
  40.4 2.7 %all-to-all-done = bf16[64,24,128]{2,1,0:T(8,128)(2,1)S(1)} async-done(((bf16[64,24,128]{2,1,0:T(8,128)(2,1)}), bf16[64,24,128]{2,1,0:T(8,128)(2,1)S(1)}, u32[]{:S(2)}, u32[]{:S(2)}) %all-to-all-start) | async-done | bytes 393248 | tf_op jit(solution)/shard_map/all_to_all | solution.py:273
  43.1 3.1 %switch.1 = (f32[2048,128]{1,0:T(8,128)S(1)}, bf16[64,2048]{1,0:T(8,128)(2,1)S(1)}) custom-call(bf16[1536,128]{1,0:T(8,128)(2,1)S(1)} %bitcast.4, bf16[8,128,128]{2,1,0:T(8,128)(2,1)S(1)} %get-tuple-element.15.weights, f32[8,128,128]{2,1,0:T(8,128)S(1)} %get-tuple-element.16.factors), custom_call_target="tpu_custom_call" | custom-call | tf_op jit(solution)/shard_map/switch/pallas_call | solution.py:233
  46.2 4.7 %collective-permute-start.2 = (bf16[64,2048]{1,0:T(8,128)(2,1)S(1)}, bf16[64,2048]{1,0:T(8,128)(2,1)S(1)}, u32[]{:S(2)}, u32[]{:S(2)}) collective-permute-start(bf16[64,2048]{1,0:T(8,128)(2,1)S(1)} %get-tuple-element.18), channel_id=1, source_target_pairs={{0,4},{1,5},{2,6},{3,7},{4,0},{5,1},{6,2},{7,3},{8,12},{9,13},{10,... | collective-permute-start | bytes 786440 | tf_op jit(solution)/shard_map/ppermute | solution.py:246
  50.9 1.3 %last.1.own = f32[64,2048]{1,0:T(8,128)S(1)} custom-call(f32[2048,128]{1,0:T(8,128)S(1)} %get-tuple-element.17.middle, bf16[8,128,128]{2,1,0:T(8,128)(2,1)S(1)} %get-tuple-element.15.weights, f32[8,128,128]{2,1,0:T(8,128)S(1)} %get-tuple-element.16.factors), custom_call_target="tpu_custom_call" | custom-call | tf_op jit(solution)/shard_map/last/pallas_call | solution.py:233
  52.2 13.9 %collective-permute-done.2.received = bf16[64,2048]{1,0:T(8,128)(2,1)S(1)} collective-permute-done((bf16[64,2048]{1,0:T(8,128)(2,1)S(1)}, bf16[64,2048]{1,0:T(8,128)(2,1)S(1)}, u32[]{:S(2)}, u32[]{:S(2)}) %collective-permute-start.2) | collective-permute-done | bytes 262176 | tf_op jit(solution)/shard_map/ppermute | solution.py:246
  66.1 0.7 %add.1 = bf16[64,2048]{1,0:T(8,128)(2,1)} custom-call(f32[64,2048]{1,0:T(8,128)S(1)} %last.1.own, bf16[64,2048]{1,0:T(8,128)(2,1)S(1)} %collective-permute-done.2.received), custom_call_target="tpu_custom_call" | custom-call | tf_op jit(solution)/shard_map/add/pallas_call | solution.py:233
  (14 shorter events, 0.1 us)
Async XLA Ops:
  0.0 1.0 %copy-start = (f32[64,2048]{1,0:T(8,128)S(1)}, f32[64,2048]{1,0:T(8,128)}, u32[]{:S(2)}) copy-start(f32[64,2048]{1,0:T(8,128)} %charges.3) | copy-start | bytes 1572868
  1.0 0.8 %copy-start.5 = (f32[64,128]{1,0:T(8,128)S(1)}, f32[64,128]{1,0:T(8,128)}, u32[]{:S(2)}) copy-start(f32[64,128]{1,0:T(8,128)} %leaf_angle.3) | copy-start | bytes 98308
  1.8 3.5 %copy-start.1 = (f32[2,96,96]{2,1,0:T(8,128)S(1)}, f32[2,96,96]{2,1,0:T(8,128)}, u32[]{:S(2)}) copy-start(f32[2,96,96]{2,1,0:T(8,128)} %level_self.3) | copy-start | bytes 221188
  1.8 3.5 %copy-start.2 = (f32[2,96,96]{2,1,0:T(8,128)S(1)}, f32[2,96,96]{2,1,0:T(8,128)}, u32[]{:S(2)}) copy-start(f32[2,96,96]{2,1,0:T(8,128)} %level_peer.3) | copy-start | bytes 221188
  1.8 3.5 %copy-start.3 = (f32[2,48,128]{2,1,0:T(8,128)S(1)}, f32[2,48,128]{2,1,0:T(8,128)}, u32[]{:S(2)}) copy-start(f32[2,48,128]{2,1,0:T(8,128)} %level_angle.3) | copy-start | bytes 147460
  1.8 3.5 %copy-start.7 = (f32[48,64]{1,0:T(8,128)S(1)}, f32[48,64]{1,0:T(8,128)}, u32[]{:S(2)}) copy-start(f32[48,64]{1,0:T(8,128)} %lagrange.1) | copy-start | bytes 36868
  1.9 10.8 %collective-permute-start = (bf16[18,64,128]{2,1,0:T(8,128)(2,1)S(1)}, bf16[18,64,128]{2,1,0:T(8,128)(2,1)S(1)}, u32[]{:S(2)}, u32[]{:S(2)}) collective-permute-start(bf16[18,64,128]{2,1,0:T(8,128)(2,1)S(1)} %pack.1), channel_id=1, source_target_pairs={{0,1},{1,0},{2,3},{3,2},{4,5},{5,4},{6,7},{7,6},{8,9},{9,8},{10,11... | collective-permute-start | bytes 884744 | tf_op jit(solution)/shard_map/ppermute | solution.py:246
  14.4 28.7 %all-to-all-start = ((bf16[64,24,128]{2,1,0:T(8,128)(2,1)}), bf16[64,24,128]{2,1,0:T(8,128)(2,1)S(1)}, u32[]{:S(2)}, u32[]{:S(2)}) async-start(bf16[64,24,128]{2,1,0:T(8,128)(2,1)} %bitcast), calls=%async_computation | async-start | bytes 786432 | tf_op jit(solution)/shard_map/all_to_all | solution.py:273
  28.2 0.8 %copy-start.4 = (f32[64,128]{1,0:T(8,128)S(1)}, f32[64,128]{1,0:T(8,128)}, u32[]{:S(2)}) copy-start(f32[64,128]{1,0:T(8,128)} %out_angle.1) | copy-start | bytes 98308
  29.0 4.9 %copy-start.9 = (f32[64,48]{0,1:T(8,128)S(1)}, f32[64,48]{0,1:T(8,128)}, u32[]{:S(2)}) copy-start(f32[64,48]{0,1:T(8,128)} %param.19) | copy-start | bytes 36868
  29.0 11.1 %copy-start.8 = (f32[48,128]{1,0:T(8,128)S(1)}, f32[48,128]{1,0:T(8,128)}, u32[]{:S(2)}) copy-start(f32[48,128]{1,0:T(8,128)} %switch_angle.1) | copy-start | bytes 73732
  29.0 11.1 %copy-start.6 = (f32[96,96]{1,0:T(8,128)S(1)}, f32[96,96]{1,0:T(8,128)}, u32[]{:S(2)}) copy-start(f32[96,96]{1,0:T(8,128)} %switch_matrix.1) | copy-start | bytes 110596
  29.0 11.0 %collective-permute-start.1 = (f32[112,128]{1,0:T(8,128)S(1)}, f32[112,128]{1,0:T(8,128)S(1)}, u32[]{:S(2)}, u32[]{:S(2)}) collective-permute-start(f32[112,128]{1,0:T(8,128)S(1)} %pad_maximum_fusion), channel_id=1, source_target_pairs={{0,4},{1,5},{2,6},{3,7},{4,0},{5,1},{6,2},{7,3},{8,12},{9,13},{10,... | collective-permute-start | bytes 172040 | tf_op jit(solution)/shard_map/ppermute | solution.py:246
  46.2 19.9 %collective-permute-start.2 = (bf16[64,2048]{1,0:T(8,128)(2,1)S(1)}, bf16[64,2048]{1,0:T(8,128)(2,1)S(1)}, u32[]{:S(2)}, u32[]{:S(2)}) collective-permute-start(bf16[64,2048]{1,0:T(8,128)(2,1)S(1)} %get-tuple-element.18), channel_id=1, source_target_pairs={{0,4},{1,5},{2,6},{3,7},{4,0},{5,1},{6,2},{7,3},{8,12},{9,13},{10,... | collective-permute-start | bytes 786440 | tf_op jit(solution)/shard_map/ppermute | solution.py:246

commit v2 on v1

--- a/solution.py
+++ b/solution.py
@@ -9,6 +9,7 @@
 BF16 = jnp.bfloat16
 LANES = 128
 CHUNK = 256
+WHOLE = 2048
 
 
 def sin_cos(angle):
@@ -45,6 +46,15 @@
     return jnp.dot(left, right, preferred_element_type=F32)
 
 
+def dot_exact(value, weights):
+    return dot(jnp.concatenate([value, value], axis=1), weights.reshape(2 * LANES, LANES))
+
+
+def dot_wide(value, weights):
+    high, low = halves(value)
+    return dot_exact(high, weights) + dot(low, weights[0])
+
+
 def dot_full(left, right, dims=((1,), (0,))):
     return lax.dot_general(
         left, right, (dims, ((), ())), precision=lax.Precision.HIGHEST, preferred_element_type=F32
@@ -85,15 +95,31 @@
     return per_box(value, cos_factor) + per_box(pltpu.roll(value, 64, 1), sin_factor)
 
 
-def pack_kernel(charges, leaf_angle, out):
-    for tile in range(16):
-        out[tile] = charges[:, tile * LANES : (tile + 1) * LANES].astype(BF16)
-    high, low = halves(leaf_angle[...])
+def pack_kernel(charges, leaf_angle, level_angle, out_angle, out, held, angle, far_angle, sems):
+    width = 512
+    copies = []
+    for step in range(2048 // width):
+        here = pl.ds(step * width, width)
+        copies.append(pltpu.make_async_copy(charges.at[:, here], held.at[:, here], sems.at[step]))
+    rest = [
+        pltpu.make_async_copy(leaf_angle, angle, sems.at[4]),
+        pltpu.make_async_copy(level_angle.at[1], far_angle.at[0:48], sems.at[5]),
+        pltpu.make_async_copy(out_angle, far_angle.at[48:112], sems.at[6]),
+    ]
+    for copy in copies + rest:
+        copy.start()
+    for step, copy in enumerate(copies):
+        copy.wait()
+        for tile in range(step * width // LANES, (step + 1) * width // LANES):
+            out[tile] = held[:, tile * LANES : (tile + 1) * LANES].astype(BF16)
+    for copy in rest:
+        copy.wait()
+    high, low = halves(angle[...])
     out[16] = high
     out[17] = low
 
 
-def source_part(read_tile, factors, weights_high, weights_low, emit):
+def source_part(read_tile, factors, weights, emit):
     for chunk in range(2048 // CHUNK):
         rows = []
         for tile in range(chunk * CHUNK // LANES, (chunk + 1) * CHUNK // LANES):
@@ -102,8 +128,7 @@
         value = jnp.concatenate(rows, axis=0)
         boxes = CHUNK // 16
         value = per_box(value, factors[chunk * boxes : (chunk + 1) * boxes, :])
-        high, low = halves(value)
-        emit(chunk, dot(high, weights_high) + dot(low, weights_high) + dot(high, weights_low))
+        emit(chunk, dot_wide(value, weights))
 
 
 def own_kernel(
@@ -118,13 +143,13 @@
     factors[0], factors[1] = rotation_factors(level_angle[0])
     sine, cosine = sin_cos(leaf_angle[...])
     turned[...] = jnp.concatenate([cosine, sine], axis=0).T
-    own_high, own_low = halves(own_weights)
+    own_weights = jnp.stack(halves(own_weights))
 
     def emit(chunk, value):
         own[chunk * CHUNK : (chunk + 1) * CHUNK, :] = value
 
     source_part(
-        lambda tile: charges[:, tile * LANES : (tile + 1) * LANES], turned, own_high, own_low, emit
+        lambda tile: charges[:, tile * LANES : (tile + 1) * LANES], turned, own_weights, emit
     )
 
 
@@ -152,7 +177,7 @@
         packed = jnp.concatenate(packed, axis=1).reshape(CHUNK * 3 // 4, LANES)
         out[chunk * CHUNK * 3 // 4 : (chunk + 1) * CHUNK * 3 // 4, :] = packed.astype(BF16)
 
-    source_part(lambda tile: received[tile].astype(F32), turned, weights[0], weights[1], emit)
+    source_part(lambda tile: received[tile].astype(F32), turned, weights[...], emit)
 
 
 def target_kernel(
@@ -176,47 +201,45 @@
 
 def evaluated(value, cos_factor, sin_factor, out_factor, weights):
     value = rotated(value, cos_factor, sin_factor)
-    high, low = halves(value)
-    value = dot(high, weights[6]) + dot(low, weights[6]) + dot(high, weights[7])
+    value = dot_wide(value, weights[6:8])
     value = per_box(value, out_factor)
     tiles = []
-    for tile in range(CHUNK // LANES):
+    for tile in range(value.shape[0] // LANES):
         turned = value[tile * LANES : (tile + 1) * LANES, :].T
         tiles.append(turned[0:64] + turned[64:128])
     return jnp.concatenate(tiles, axis=1)
 
 
 def switch_kernel(received, weights, factors, middle, sent):
-    lane = lax.broadcasted_iota(jnp.int32, (CHUNK // 4, LANES), 1) % 64
-    boxes = CHUNK // 16
-    for chunk in range(2048 // CHUNK):
-        packed = received[chunk * CHUNK * 3 // 4 : (chunk + 1) * CHUNK * 3 // 4, :].astype(F32)
-        parts = packed.reshape(CHUNK // 32, 3, 8, LANES)
-        first = [parts[:, i].reshape(CHUNK // 4, LANES) for i in range(3)]
+    lane = lax.broadcasted_iota(jnp.int32, (WHOLE // 4, LANES), 1) % 64
+    boxes = WHOLE // 16
+    for chunk in range(2048 // WHOLE):
+        packed = received[chunk * WHOLE * 3 // 4 : (chunk + 1) * WHOLE * 3 // 4, :].astype(F32)
+        parts = packed.reshape(WHOLE // 32, 3, 8, LANES)
+        first = [parts[:, i].reshape(WHOLE // 4, LANES) for i in range(3)]
         last = jnp.where(
             lane < 16,
             pltpu.roll(first[0], 80, 1),
             jnp.where(lane < 32, pltpu.roll(first[1], 96, 1), pltpu.roll(first[2], 112, 1)),
         )
         value = jnp.concatenate(
-            [part.reshape(CHUNK // 32, 1, 8, LANES) for part in first + [last]], axis=1
-        ).reshape(CHUNK, LANES)
+            [part.reshape(WHOLE // 32, 1, 8, LANES) for part in first + [last]], axis=1
+        ).reshape(WHOLE, LANES)
         value = value.astype(BF16)
-        value = dot(value, weights[0]) + dot(value, weights[1])
+        value = dot_exact(value, weights[0:2])
         here = pl.ds(chunk * boxes, boxes)
         value = rotated(value, factors[0, here, :], factors[1, here, :])
-        middle[chunk * CHUNK : (chunk + 1) * CHUNK, :] = value
+        middle[chunk * WHOLE : (chunk + 1) * WHOLE, :] = value
         value = value.astype(BF16)
-        value = dot(value, weights[2]) + dot(value, weights[3])
+        value = dot_exact(value, weights[2:4])
         value = evaluated(value, factors[5, here, :], factors[6, here, :], factors[7, here, :], weights)
-        sent[:, chunk * CHUNK : (chunk + 1) * CHUNK] = value.astype(BF16)
+        sent[:, chunk * WHOLE : (chunk + 1) * WHOLE] = value.astype(BF16)
 
 
 def last_kernel(middle, weights, factors, own):
     boxes = CHUNK // 16
     for chunk in range(2048 // CHUNK):
-        high, low = halves(middle[chunk * CHUNK : (chunk + 1) * CHUNK, :])
-        value = dot(high, weights[4]) + dot(low, weights[4]) + dot(high, weights[5])
+        value = dot_wide(middle[chunk * CHUNK : (chunk + 1) * CHUNK, :], weights[4:6])
         here = pl.ds(chunk * boxes, boxes)
         own[:, chunk * CHUNK : (chunk + 1) * CHUNK] = evaluated(
             value, factors[2, here, :], factors[3, here, :], factors[4, here, :], weights
@@ -227,15 +250,16 @@
     out[...] = (own[...] + received[...].astype(F32)).astype(BF16)
 
 
-def call(kernel, outs, args, scratch=(), name=None):
+def call(kernel, outs, args, scratch=(), name=None, hbm=False):
     whole = pl.BlockSpec(memory_space=pltpu.VMEM)
+    source = pl.BlockSpec(memory_space=pltpu.HBM) if hbm else whole
     shapes = [jax.ShapeDtypeStruct(shape, dtype) for shape, dtype in outs]
     return pl.pallas_call(
         kernel,
         out_shape=shapes if len(shapes) > 1 else shapes[0],
-        in_specs=[whole] * len(args),
+        in_specs=[source] * len(args),
         out_specs=[whole] * len(shapes) if len(shapes) > 1 else whole,
-        scratch_shapes=[pltpu.VMEM((LANES, LANES), F32)] * scratch if scratch else [],
+        scratch_shapes=scratch,
         compiler_params=pltpu.CompilerParams(vmem_limit_bytes=32 * 1024 * 1024),
         name=name,
     )(*args)
@@ -259,23 +283,32 @@
     evaluate,
 ):
     square = (LANES, LANES)
-    packed = call(pack_kernel, [((18, 64, LANES), BF16)], [charges, leaf_angle], name="pack")
+    tile = pltpu.VMEM(square, F32)
+    packed, charges, leaf_angle, far_angle = call(
+        pack_kernel,
+        [((18, 64, LANES), BF16), ((64, 2048), F32), ((64, LANES), F32), ((112, LANES), F32)],
+        [pltpu.with_memory_space_constraint(x, pltpu.HBM) for x in (charges, leaf_angle, level_angle, out_angle)],
+        [pltpu.SemaphoreType.DMA((7,))],
+        name="pack",
+        hbm=True,
+    )
     near = from_partner(packed, 1)
-    far_angle = from_partner(jnp.concatenate([level_angle[1], out_angle], axis=0), 4)
+    far_angle = from_partner(far_angle, 4)
     own, weights, factors = call(
         own_kernel,
         [((2048, LANES), F32), ((2, *square), BF16), ((2, *square), F32)],
         [charges, leaf_angle, lagrange, level_angle, level_self, level_peer],
-        2,
+        [tile] * 2,
         name="own",
     )
-    state = call(peer_kernel, [((1536, LANES), BF16)], [near, own, weights, factors], 1, name="peer")
+    near, far_angle = lax.optimization_barrier((near, far_angle))
+    state = call(peer_kernel, [((1536, LANES), BF16)], [near, own, weights, factors], [tile], name="peer")
     state = lax.all_to_all(state.reshape(64, 24, LANES), "wide", 0, 0, tiled=True).reshape(1536, LANES)
     weights, factors = call(
         target_kernel,
         [((8, *square), BF16), ((8, *square), F32)],
         [level_angle, far_angle, switch_angle, out_angle, level_self, level_peer, switch_matrix, evaluate],
-        1,
+        [tile],
         name="target",
     )
     middle, sent = call(

time: 67.4 us -> 71.8 us (1.065)
  the two profiles are of different devices: /device:TPU:56 before, /device:TPU:9 now
where the time goes in v2:
time: 71.8 us; the launch traced here: 71.5 us
  waiting for transfers between devices  33.8 us (47%)
  starting transfers between devices  28.6 us (40%)
  Pallas kernels  8.18 us (11%)
  local copies, waits for them, and re-layouts  0.76 us (1%)
    ppermute x3, waiting for transfers between devices, from_partner(): return lax.ppermute(value, 'narrow', pairs)  19.9 us
    all_to_all x1, starting transfers between devices, body(): lax.all_to_all(state.reshape(64, 24, LANES), 'wide', 0, 0, tiled=True)  15.9 us
    all_to_all x1, waiting for transfers between devices, body(): lax.all_to_all(state.reshape(64, 24, LANES), 'wide', 0, 0, tiled=True)  13.9 us
    ppermute x3, starting transfers between devices, from_partner(): return lax.ppermute(value, 'narrow', pairs)  12.6 us
    pallas_call x7, Pallas kernels, call(): pl.pallas_call(kernel, out_shape=shapes if len(shapes) > 1 else shapes[0]...  8.18 us
  transfers between devices with their start and end apart: 4, of which 3 were waited for; matrix products, arithmetic and copies ran while one was open for 0% of the time, Pallas kernels for 4%

profile of v2, /device:TPU:9, one launch (start us, length us, event | category | flops | bytes accessed | tf_op | source)
XLA Modules:
  0.0 71.5 jit_solution(8234637464272457327)
XLA Ops:
  0.0 0.0 copy-start.5
  0.0 1.2 %pack.1 = (bf16[18,64,128]{2,1,0:T(8,128)(2,1)S(1)}, f32[64,2048]{1,0:T(8,128)S(1)}, f32[64,128]{1,0:T(8,128)S(1)}, f32[112,128]{1,0:T(8,128)S(1)}) custom-call(f32[64,2048]{1,0:T(8,128)} %charges.1, f32[64,128]{1,0:T(8,128)} %leaf_angle.1, f32[2,48,128]{2,1,0:T(8,128)} %level_angle.5, f32[64,128]{1,0:T(8,128)} %out_angle.3), custom_call_target="tpu_custom_call" | custom-call | tf_op jit(solution)/shard_map/pack/pallas_call | solution.py:257
  1.2 1.9 %collective-permute-start = (bf16[18,64,128]{2,1,0:T(8,128)(2,1)S(1)}, bf16[18,64,128]{2,1,0:T(8,128)(2,1)S(1)}, u32[]{:S(2)}, u32[]{:S(2)}) collective-permute-start(bf16[18,64,128]{2,1,0:T(8,128)(2,1)S(1)} %get-tuple-element.18), channel_id=1, source_target_pairs={{0,1},{1,0},{2,3},{3,2},{4,5},{5,4},{6,7},{7,6},{8,9},{9,8},{10,11... | collective-permute-start | bytes 884744 | tf_op jit(solution)/shard_map/ppermute | solution.py:270
  3.2 7.6 %collective-permute-start.1 = (f32[112,128]{1,0:T(8,128)S(1)}, f32[112,128]{1,0:T(8,128)S(1)}, u32[]{:S(2)}, u32[]{:S(2)}) collective-permute-start(f32[112,128]{1,0:T(8,128)S(1)} %get-tuple-element.19), channel_id=1, source_target_pairs={{0,4},{1,5},{2,6},{3,7},{4,0},{5,1},{6,2},{7,3},{8,12},{9,13},{10,... | collective-permute-start | bytes 172040 | tf_op jit(solution)/shard_map/ppermute | solution.py:270
  10.8 0.0 copy-done
  10.8 0.0 copy-done.1
  10.8 0.0 copy-done.2
  10.8 0.0 copy-done.5
  10.8 1.0 %own.1 = (f32[2048,128]{1,0:T(8,128)S(1)}, bf16[2,128,128]{2,1,0:T(8,128)(2,1)S(1)}, f32[2,128,128]{2,1,0:T(8,128)S(1)}) custom-call(f32[64,2048]{1,0:T(8,128)S(1)} %get-tuple-element.21.charges, f32[64,128]{1,0:T(8,128)S(1)} %get-tuple-element.22.leaf_angle, f32[48,64]{1,0:T(8,128)S(1)} %copy-done.5, f32[2,48,128]{2,1,0:T(8,128)S(1)} %copy-done, ...), custom_call_target="tpu_custom_call" | custom-call | tf_op jit(solution)/shard_map/own/pallas_call | solution.py:257
  11.9 5.0 %collective-permute-done.1.peer_angle = f32[112,128]{1,0:T(8,128)S(1)} collective-permute-done((f32[112,128]{1,0:T(8,128)S(1)}, f32[112,128]{1,0:T(8,128)S(1)}, u32[]{:S(2)}, u32[]{:S(2)}) %collective-permute-start.1) | collective-permute-done | bytes 57376 | tf_op jit(solution)/shard_map/ppermute | solution.py:270
  16.8 0.0 collective-permute-done.received
  16.8 1.8 %peer.1 = bf16[1536,128]{1,0:T(8,128)(2,1)} custom-call(bf16[18,64,128]{2,1,0:T(8,128)(2,1)S(1)} %collective-permute-done.received, f32[2048,128]{1,0:T(8,128)S(1)} %get-tuple-element.23.own, bf16[2,128,128]{2,1,0:T(8,128)(2,1)S(1)} %get-tuple-element.24.weights, f32[2,128,128]{2,1,0:T(8,128)S(1)} %get-tuple-element.25.factors), custom_call_target="tpu_custom_call" | custom-call | tf_op jit(solution)/shard_map/peer/pallas_call | solution.py:257
  18.6 15.9 %all-to-all-start = ((bf16[64,24,128]{2,1,0:T(8,128)(2,1)}), bf16[64,24,128]{2,1,0:T(8,128)(2,1)S(1)}, u32[]{:S(2)}, u32[]{:S(2)}) async-start(bf16[64,24,128]{2,1,0:T(8,128)(2,1)} %bitcast), calls=%async_computation | async-start | bytes 786432 | tf_op jit(solution)/shard_map/all_to_all | solution.py:306
  34.5 0.0 copy-start.3
  34.6 0.0 copy-start.6
  34.6 0.1 copy.11.evaluate
  34.6 0.7 copy-done.3
  35.3 0.4 target.1
  35.7 13.9 %all-to-all-done = bf16[64,24,128]{2,1,0:T(8,128)(2,1)S(1)} async-done(((bf16[64,24,128]{2,1,0:T(8,128)(2,1)}), bf16[64,24,128]{2,1,0:T(8,128)(2,1)S(1)}, u32[]{:S(2)}, u32[]{:S(2)}) %all-to-all-start) | async-done | bytes 393248 | tf_op jit(solution)/shard_map/all_to_all | solution.py:306
  49.6 1.7 %switch.1 = (f32[2048,128]{1,0:T(8,128)S(1)}, bf16[64,2048]{1,0:T(8,128)(2,1)S(1)}) custom-call(bf16[1536,128]{1,0:T(8,128)(2,1)S(1)} %bitcast.2, bf16[8,128,128]{2,1,0:T(8,128)(2,1)S(1)} %get-tuple-element.27.weights, f32[8,128,128]{2,1,0:T(8,128)S(1)} %get-tuple-element.28.factors), custom_call_target="tpu_custom_call" | custom-call | tf_op jit(solution)/shard_map/switch/pallas_call | solution.py:257
  51.3 3.1 %collective-permute-start.2 = (bf16[64,2048]{1,0:T(8,128)(2,1)S(1)}, bf16[64,2048]{1,0:T(8,128)(2,1)S(1)}, u32[]{:S(2)}, u32[]{:S(2)}) collective-permute-start(bf16[64,2048]{1,0:T(8,128)(2,1)S(1)} %get-tuple-element.30), channel_id=1, source_target_pairs={{0,4},{1,5},{2,6},{3,7},{4,0},{5,1},{6,2},{7,3},{8,12},{9,13},{10,... | collective-permute-start | bytes 786440 | tf_op jit(solution)/shard_map/ppermute | solution.py:270
  54.5 1.3 %last.1.own = f32[64,2048]{1,0:T(8,128)S(1)} custom-call(f32[2048,128]{1,0:T(8,128)S(1)} %get-tuple-element.29.middle, bf16[8,128,128]{2,1,0:T(8,128)(2,1)S(1)} %get-tuple-element.27.weights, f32[8,128,128]{2,1,0:T(8,128)S(1)} %get-tuple-element.28.factors), custom_call_target="tpu_custom_call" | custom-call | tf_op jit(solution)/shard_map/last/pallas_call | solution.py:257
  55.8 15.0 %collective-permute-done.2.received = bf16[64,2048]{1,0:T(8,128)(2,1)S(1)} collective-permute-done((bf16[64,2048]{1,0:T(8,128)(2,1)S(1)}, bf16[64,2048]{1,0:T(8,128)(2,1)S(1)}, u32[]{:S(2)}, u32[]{:S(2)}) %collective-permute-start.2) | collective-permute-done | bytes 262176 | tf_op jit(solution)/shard_map/ppermute | solution.py:270
  70.7 0.7 %add.1 = bf16[64,2048]{1,0:T(8,128)(2,1)} custom-call(f32[64,2048]{1,0:T(8,128)S(1)} %last.1.own, bf16[64,2048]{1,0:T(8,128)(2,1)S(1)} %collective-permute-done.2.received), custom_call_target="tpu_custom_call" | custom-call | tf_op jit(solution)/shard_map/add/pallas_call | solution.py:257
  (8 shorter events, 0.0 us)
Async XLA Ops:
  0.0 10.8 %copy-start = (f32[2,48,128]{2,1,0:T(8,128)S(1)}, f32[2,48,128]{2,1,0:T(8,128)}, u32[]{:S(2)}) copy-start(f32[2,48,128]{2,1,0:T(8,128)} %level_angle.5) | copy-start | bytes 147460
  0.0 10.8 %copy-start.1 = (f32[2,96,96]{2,1,0:T(8,128)S(1)}, f32[2,96,96]{2,1,0:T(8,128)}, u32[]{:S(2)}) copy-start(f32[2,96,96]{2,1,0:T(8,128)} %level_self.3) | copy-start | bytes 221188
  0.0 10.8 %copy-start.2 = (f32[2,96,96]{2,1,0:T(8,128)S(1)}, f32[2,96,96]{2,1,0:T(8,128)}, u32[]{:S(2)}) copy-start(f32[2,96,96]{2,1,0:T(8,128)} %level_peer.3) | copy-start | bytes 221188
  0.0 10.8 %copy-start.5 = (f32[48,64]{1,0:T(8,128)S(1)}, f32[48,64]{1,0:T(8,128)}, u32[]{:S(2)}) copy-start(f32[48,64]{1,0:T(8,128)} %lagrange.1) | copy-start | bytes 36868
  1.2 15.6 %collective-permute-start = (bf16[18,64,128]{2,1,0:T(8,128)(2,1)S(1)}, bf16[18,64,128]{2,1,0:T(8,128)(2,1)S(1)}, u32[]{:S(2)}, u32[]{:S(2)}) collective-permute-start(bf16[18,64,128]{2,1,0:T(8,128)(2,1)S(1)} %get-tuple-element.18), channel_id=1, source_target_pairs={{0,1},{1,0},{2,3},{3,2},{4,5},{5,4},{6,7},{7,6},{8,9},{9,8},{10,11... | collective-permute-start | bytes 884744 | tf_op jit(solution)/shard_map/ppermute | solution.py:270
  3.2 13.6 %collective-permute-start.1 = (f32[112,128]{1,0:T(8,128)S(1)}, f32[112,128]{1,0:T(8,128)S(1)}, u32[]{:S(2)}, u32[]{:S(2)}) collective-permute-start(f32[112,128]{1,0:T(8,128)S(1)} %get-tuple-element.19), channel_id=1, source_target_pairs={{0,4},{1,5},{2,6},{3,7},{4,0},{5,1},{6,2},{7,3},{8,12},{9,13},{10,... | collective-permute-start | bytes 172040 | tf_op jit(solution)/shard_map/ppermute | solution.py:270
  18.6 15.9 %copy-start.7 = (f32[64,48]{0,1:T(8,128)S(1)}, f32[64,48]{0,1:T(8,128)}, u32[]{:S(2)}) copy-start(f32[64,48]{0,1:T(8,128)} %param.19) | copy-start | bytes 36868
  18.6 16.0 %copy-start.4 = (f32[96,96]{1,0:T(8,128)S(1)}, f32[96,96]{1,0:T(8,128)}, u32[]{:S(2)}) copy-start(f32[96,96]{1,0:T(8,128)} %switch_matrix.1) | copy-start | bytes 110596
  18.6 31.0 %all-to-all-start = ((bf16[64,24,128]{2,1,0:T(8,128)(2,1)}), bf16[64,24,128]{2,1,0:T(8,128)(2,1)S(1)}, u32[]{:S(2)}, u32[]{:S(2)}) async-start(bf16[64,24,128]{2,1,0:T(8,128)(2,1)} %bitcast), calls=%async_computation | async-start | bytes 786432 | tf_op jit(solution)/shard_map/all_to_all | solution.py:306
  34.5 0.8 %copy-start.3 = (f32[64,128]{1,0:T(8,128)S(1)}, f32[64,128]{1,0:T(8,128)}, u32[]{:S(2)}) copy-start(f32[64,128]{1,0:T(8,128)} %out_angle.3) | copy-start | bytes 98308
  34.6 0.8 %copy-start.6 = (f32[48,128]{1,0:T(8,128)S(1)}, f32[48,128]{1,0:T(8,128)}, u32[]{:S(2)}) copy-start(f32[48,128]{1,0:T(8,128)} %switch_angle.1) | copy-start | bytes 73732
  51.3 19.4 %collective-permute-start.2 = (bf16[64,2048]{1,0:T(8,128)(2,1)S(1)}, bf16[64,2048]{1,0:T(8,128)(2,1)S(1)}, u32[]{:S(2)}, u32[]{:S(2)}) collective-permute-start(bf16[64,2048]{1,0:T(8,128)(2,1)S(1)} %get-tuple-element.30), channel_id=1, source_target_pairs={{0,4},{1,5},{2,6},{3,7},{4,0},{5,1},{6,2},{7,3},{8,12},{9,13},{10,... | collective-permute-start | bytes 786440 | tf_op jit(solution)/shard_map/ppermute | solution.py:270

commit v3 on v2

--- a/solution.py
+++ b/solution.py
@@ -8,7 +8,7 @@
 F32 = jnp.float32
 BF16 = jnp.bfloat16
 LANES = 128
-CHUNK = 256
+CHUNK = 1024
 WHOLE = 2048
 
 
@@ -46,13 +46,24 @@
     return jnp.dot(left, right, preferred_element_type=F32)
 
 
+def wide_weights(matrix):
+    high, low = halves(matrix)
+    return jnp.concatenate(
+        [jnp.concatenate([high, low], axis=1), jnp.concatenate([high, jnp.zeros_like(low)], axis=1)], axis=0
+    )
+
+
+def tall_weights(matrix):
+    return jnp.concatenate(halves(matrix), axis=0)
+
+
 def dot_exact(value, weights):
-    return dot(jnp.concatenate([value, value], axis=1), weights.reshape(2 * LANES, LANES))
+    return dot(jnp.concatenate([value, value], axis=1), weights)
 
 
 def dot_wide(value, weights):
-    high, low = halves(value)
-    return dot_exact(high, weights) + dot(low, weights[0])
+    both = dot(jnp.concatenate(halves(value), axis=1), weights)
+    return both[:, :LANES] + both[:, LANES:]
 
 
 def dot_full(left, right, dims=((1,), (0,))):
@@ -139,11 +150,11 @@
     own_weights = dot_full(leaf, self_matrix, ((0,), (1,)))
     peer_matrix = spread(level_peer.at[0], scratch)
     peer_weights = dot_full(leaf, peer_matrix, ((0,), (1,)))
-    weights[0], weights[1] = halves(peer_weights)
+    weights[...] = wide_weights(peer_weights)
     factors[0], factors[1] = rotation_factors(level_angle[0])
     sine, cosine = sin_cos(leaf_angle[...])
     turned[...] = jnp.concatenate([cosine, sine], axis=0).T
-    own_weights = jnp.stack(halves(own_weights))
+    own_weights = wide_weights(own_weights)
 
     def emit(chunk, value):
         own[chunk * CHUNK : (chunk + 1) * CHUNK, :] = value
@@ -181,15 +192,15 @@
 
 
 def target_kernel(
-    level_angle, peer_angle, switch_angle, out_angle, level_self, level_peer, switch_matrix, evaluate, weights, factors, scratch
+    level_angle, peer_angle, switch_angle, out_angle, level_self, level_peer, switch_matrix, evaluate, tall, wide, factors, scratch
 ):
-    weights[0], weights[1] = halves(spread(switch_matrix, scratch).T)
-    weights[2], weights[3] = halves(spread(level_peer.at[1], scratch).T)
-    weights[4], weights[5] = halves(spread(level_self.at[1], scratch).T)
+    tall[0] = tall_weights(spread(switch_matrix, scratch).T)
+    tall[1] = tall_weights(spread(level_peer.at[1], scratch).T)
+    wide[0] = wide_weights(spread(level_self.at[1], scratch).T)
     scratch[...] = jnp.zeros((LANES, LANES), F32)
     scratch[0:64, 0:48] = evaluate[...]
     scratch[64:128, 64:112] = evaluate[...]
-    weights[6], weights[7] = halves(scratch[...].T)
+    wide[1] = wide_weights(scratch[...].T)
     factors[0], factors[1] = rotation_factors(switch_angle[...])
     factors[2], factors[3] = rotation_factors(level_angle[1])
     sine, cosine = sin_cos(out_angle[...])
@@ -199,9 +210,9 @@
     factors[7] = jnp.concatenate([cosine, -sine], axis=0).T
 
 
-def evaluated(value, cos_factor, sin_factor, out_factor, weights):
+def evaluated(value, cos_factor, sin_factor, out_factor, last_weights):
     value = rotated(value, cos_factor, sin_factor)
-    value = dot_wide(value, weights[6:8])
+    value = dot_wide(value, last_weights)
     value = per_box(value, out_factor)
     tiles = []
     for tile in range(value.shape[0] // LANES):
@@ -210,7 +221,7 @@
     return jnp.concatenate(tiles, axis=1)
 
 
-def switch_kernel(received, weights, factors, middle, sent):
+def switch_kernel(received, tall, wide, factors, middle, sent):
     lane = lax.broadcasted_iota(jnp.int32, (WHOLE // 4, LANES), 1) % 64
     boxes = WHOLE // 16
     for chunk in range(2048 // WHOLE):
@@ -226,23 +237,23 @@
             [part.reshape(WHOLE // 32, 1, 8, LANES) for part in first + [last]], axis=1
         ).reshape(WHOLE, LANES)
         value = value.astype(BF16)
-        value = dot_exact(value, weights[0:2])
+        value = dot_exact(value, tall[0])
         here = pl.ds(chunk * boxes, boxes)
         value = rotated(value, factors[0, here, :], factors[1, here, :])
         middle[chunk * WHOLE : (chunk + 1) * WHOLE, :] = value
         value = value.astype(BF16)
-        value = dot_exact(value, weights[2:4])
-        value = evaluated(value, factors[5, here, :], factors[6, here, :], factors[7, here, :], weights)
+        value = dot_exact(value, tall[1])
+        value = evaluated(value, factors[5, here, :], factors[6, here, :], factors[7, here, :], wide[1])
         sent[:, chunk * WHOLE : (chunk + 1) * WHOLE] = value.astype(BF16)
 
 
-def last_kernel(middle, weights, factors, own):
+def last_kernel(middle, wide, factors, own):
     boxes = CHUNK // 16
     for chunk in range(2048 // CHUNK):
-        value = dot_wide(middle[chunk * CHUNK : (chunk + 1) * CHUNK, :], weights[4:6])
+        value = dot_wide(middle[chunk * CHUNK : (chunk + 1) * CHUNK, :], wide[0])
         here = pl.ds(chunk * boxes, boxes)
         own[:, chunk * CHUNK : (chunk + 1) * CHUNK] = evaluated(
-            value, factors[2, here, :], factors[3, here, :], factors[4, here, :], weights
+            value, factors[2, here, :], factors[3, here, :], factors[4, here, :], wide[1]
         )
 
 
@@ -296,17 +307,16 @@
     far_angle = from_partner(far_angle, 4)
     own, weights, factors = call(
         own_kernel,
-        [((2048, LANES), F32), ((2, *square), BF16), ((2, *square), F32)],
+        [((2048, LANES), F32), ((2 * LANES, 2 * LANES), BF16), ((2, *square), F32)],
         [charges, leaf_angle, lagrange, level_angle, level_self, level_peer],
         [tile] * 2,
         name="own",
     )
-    near, far_angle = lax.optimization_barrier((near, far_angle))
     state = call(peer_kernel, [((1536, LANES), BF16)], [near, own, weights, factors], [tile], name="peer")
     state = lax.all_to_all(state.reshape(64, 24, LANES), "wide", 0, 0, tiled=True).reshape(1536, LANES)
-    weights, factors = call(
+    tall, wide, factors = call(
         target_kernel,
-        [((8, *square), BF16), ((8, *square), F32)],
+        [((2, 2 * LANES, LANES), BF16), ((2, 2 * LANES, 2 * LANES), BF16), ((8, *square), F32)],
         [level_angle, far_angle, switch_angle, out_angle, level_self, level_peer, switch_matrix, evaluate],
         [tile],
         name="target",
@@ -314,11 +324,11 @@
     middle, sent = call(
         switch_kernel,
         [((2048, LANES), F32), ((64, 2048), BF16)],
-        [state, weights, factors],
+        [state, tall, wide, factors],
         name="switch",
     )
     far = from_partner(sent, 4)
-    own = call(last_kernel, [((64, 2048), F32)], [middle, weights, factors], name="last")
+    own = call(last_kernel, [((64, 2048), F32)], [middle, wide, factors], name="last")
     return call(add_kernel, [((64, 2048), BF16)], [own, far], name="add")
 
 

time: 71.8 us -> 65 us (0.905)
  the two profiles are of different devices: /device:TPU:9 before, /device:TPU:56 now
where the time goes in v3:
time: 65 us; the launch traced here: 64.6 us
  waiting for transfers between devices  30.1 us (46%)
  starting transfers between devices  26.6 us (41%)
  Pallas kernels  7.57 us (12%)
    ppermute x3, waiting for transfers between devices, from_partner(): return lax.ppermute(value, 'narrow', pairs)  26.6 us
    all_to_all x1, starting transfers between devices, body(): lax.all_to_all(state.reshape(64, 24, LANES), 'wide', 0, 0, tiled=True)  13.9 us
    ppermute x3, starting transfers between devices, from_partner(): return lax.ppermute(value, 'narrow', pairs)  12.7 us
    pallas_call x7, Pallas kernels, call(): pl.pallas_call(kernel, out_shape=shapes if len(shapes) > 1 else shapes[0]...  7.57 us
    all_to_all x1, waiting for transfers between devices, body(): lax.all_to_all(state.reshape(64, 24, LANES), 'wide', 0, 0, tiled=True)  3.54 us
  transfers between devices with their start and end apart: 4, of which 4 were waited for; matrix products, arithmetic and copies ran while one was open for 0% of the time, Pallas kernels for 4%

profile of v3, /device:TPU:56, one launch (start us, length us, event | category | flops | bytes accessed | tf_op | source)
XLA Modules:
  0.0 64.6 jit_solution(10416538690711576816)
XLA Ops:
  0.0 0.0 copy-start.2
  0.0 1.2 %pack.1 = (bf16[18,64,128]{2,1,0:T(8,128)(2,1)S(1)}, f32[64,2048]{1,0:T(8,128)S(1)}, f32[64,128]{1,0:T(8,128)S(1)}, f32[112,128]{1,0:T(8,128)S(1)}) custom-call(f32[64,2048]{1,0:T(8,128)} %charges.1, f32[64,128]{1,0:T(8,128)} %leaf_angle.1, f32[2,48,128]{2,1,0:T(8,128)} %level_angle.5, f32[64,128]{1,0:T(8,128)} %out_angle.3), custom_call_target="tpu_custom_call" | custom-call | tf_op jit(solution)/shard_map/pack/pallas_call | solution.py:268
  1.2 3.3 %collective-permute-start = (bf16[18,64,128]{2,1,0:T(8,128)(2,1)S(1)}, bf16[18,64,128]{2,1,0:T(8,128)(2,1)S(1)}, u32[]{:S(2)}, u32[]{:S(2)}) collective-permute-start(bf16[18,64,128]{2,1,0:T(8,128)(2,1)S(1)} %get-tuple-element.17), channel_id=1, source_target_pairs={{0,1},{1,0},{2,3},{3,2},{4,5},{5,4},{6,7},{7,6},{8,9},{9,8},{10,11... | collective-permute-start | bytes 884744 | tf_op jit(solution)/shard_map/ppermute | solution.py:281
  4.5 0.0 copy-done
  4.5 0.0 copy-done.5
  4.5 0.0 copy-done.1
  4.5 0.0 copy-done.2
  4.6 0.9 %own.1 = (f32[2048,128]{1,0:T(8,128)S(1)}, bf16[256,256]{1,0:T(8,128)(2,1)S(1)}, f32[2,128,128]{2,1,0:T(8,128)S(1)}) custom-call(f32[64,2048]{1,0:T(8,128)S(1)} %get-tuple-element.18.charges, f32[64,128]{1,0:T(8,128)S(1)} %get-tuple-element.19.leaf_angle, f32[48,64]{1,0:T(8,128)S(1)} %copy-done.5, f32[2,48,128]{2,1,0:T(8,128)S(1)} %copy-done, ...), custom_call_target="tpu_custom_call" | custom-call | tf_op jit(solution)/shard_map/own/pallas_call | solution.py:268
  5.5 6.4 %collective-permute-done.received = bf16[18,64,128]{2,1,0:T(8,128)(2,1)S(1)} collective-permute-done((bf16[18,64,128]{2,1,0:T(8,128)(2,1)S(1)}, bf16[18,64,128]{2,1,0:T(8,128)(2,1)S(1)}, u32[]{:S(2)}, u32[]{:S(2)}) %collective-permute-start) | collective-permute-done | bytes 294944 | tf_op jit(solution)/shard_map/ppermute | solution.py:281
  11.9 1.6 %peer.1 = bf16[1536,128]{1,0:T(8,128)(2,1)} custom-call(bf16[18,64,128]{2,1,0:T(8,128)(2,1)S(1)} %collective-permute-done.received, f32[2048,128]{1,0:T(8,128)S(1)} %get-tuple-element.20.own, bf16[256,256]{1,0:T(8,128)(2,1)S(1)} %get-tuple-element.21.weights, f32[2,128,128]{2,1,0:T(8,128)S(1)} %get-tuple-element.22.factors), custom_call_target="tpu_custom_call" | custom-call | tf_op jit(solution)/shard_map/peer/pallas_call | solution.py:268
  13.5 13.9 %all-to-all-start = ((bf16[64,24,128]{2,1,0:T(8,128)(2,1)}), bf16[64,24,128]{2,1,0:T(8,128)(2,1)S(1)}, u32[]{:S(2)}, u32[]{:S(2)}) async-start(bf16[64,24,128]{2,1,0:T(8,128)(2,1)} %bitcast), calls=%async_computation | async-start | bytes 786432 | tf_op jit(solution)/shard_map/all_to_all | solution.py:316
  27.4 0.0 copy-start.3
  27.4 0.0 copy-start.6
  27.5 4.7 %collective-permute-start.1 = (f32[112,128]{1,0:T(8,128)S(1)}, f32[112,128]{1,0:T(8,128)S(1)}, u32[]{:S(2)}, u32[]{:S(2)}) collective-permute-start(f32[112,128]{1,0:T(8,128)S(1)} %get-tuple-element.23), channel_id=1, source_target_pairs={{0,4},{1,5},{2,6},{3,7},{4,0},{5,1},{6,2},{7,3},{8,12},{9,13},{10,... | collective-permute-start | bytes 172040 | tf_op jit(solution)/shard_map/ppermute | solution.py:281
  32.2 0.0 copy-done.7
  32.2 0.1 copy.11.evaluate
  32.3 6.1 %collective-permute-done.1.peer_angle = f32[112,128]{1,0:T(8,128)S(1)} collective-permute-done((f32[112,128]{1,0:T(8,128)S(1)}, f32[112,128]{1,0:T(8,128)S(1)}, u32[]{:S(2)}, u32[]{:S(2)}) %collective-permute-start.1) | collective-permute-done | bytes 57376 | tf_op jit(solution)/shard_map/ppermute | solution.py:281
  38.4 0.4 target.1
  38.8 3.5 %all-to-all-done = bf16[64,24,128]{2,1,0:T(8,128)(2,1)S(1)} async-done(((bf16[64,24,128]{2,1,0:T(8,128)(2,1)}), bf16[64,24,128]{2,1,0:T(8,128)(2,1)S(1)}, u32[]{:S(2)}, u32[]{:S(2)}) %all-to-all-start) | async-done | bytes 393248 | tf_op jit(solution)/shard_map/all_to_all | solution.py:316
  42.3 1.6 %switch.1 = (f32[2048,128]{1,0:T(8,128)S(1)}, bf16[64,2048]{1,0:T(8,128)(2,1)S(1)}) custom-call(bf16[1536,128]{1,0:T(8,128)(2,1)S(1)} %bitcast.2, bf16[2,256,128]{2,1,0:T(8,128)(2,1)S(1)} %get-tuple-element.24.tall, bf16[2,256,256]{2,1,0:T(8,128)(2,1)S(1)} %get-tuple-element.25.wide, f32[8,128,128]{2,1,0:T(8,128)S(1)} %get-tuple-element.26.factors), custom_call_target="tpu_custom_call" | custom-call | tf_op jit(solution)/shard_map/switch/pallas_call | solution.py:268
  43.9 4.7 %collective-permute-start.2 = (bf16[64,2048]{1,0:T(8,128)(2,1)S(1)}, bf16[64,2048]{1,0:T(8,128)(2,1)S(1)}, u32[]{:S(2)}, u32[]{:S(2)}) collective-permute-start(bf16[64,2048]{1,0:T(8,128)(2,1)S(1)} %get-tuple-element.28), channel_id=1, source_target_pairs={{0,4},{1,5},{2,6},{3,7},{4,0},{5,1},{6,2},{7,3},{8,12},{9,13},{10,... | collective-permute-start | bytes 786440 | tf_op jit(solution)/shard_map/ppermute | solution.py:281
  48.6 1.1 %last.1.own = f32[64,2048]{1,0:T(8,128)S(1)} custom-call(f32[2048,128]{1,0:T(8,128)S(1)} %get-tuple-element.27.middle, bf16[2,256,256]{2,1,0:T(8,128)(2,1)S(1)} %get-tuple-element.25.wide, f32[8,128,128]{2,1,0:T(8,128)S(1)} %get-tuple-element.26.factors), custom_call_target="tpu_custom_call" | custom-call | tf_op jit(solution)/shard_map/last/pallas_call | solution.py:268
  49.7 14.1 %collective-permute-done.2.received = bf16[64,2048]{1,0:T(8,128)(2,1)S(1)} collective-permute-done((bf16[64,2048]{1,0:T(8,128)(2,1)S(1)}, bf16[64,2048]{1,0:T(8,128)(2,1)S(1)}, u32[]{:S(2)}, u32[]{:S(2)}) %collective-permute-start.2) | collective-permute-done | bytes 262176 | tf_op jit(solution)/shard_map/ppermute | solution.py:281
  63.8 0.7 %add.1 = bf16[64,2048]{1,0:T(8,128)(2,1)} custom-call(f32[64,2048]{1,0:T(8,128)S(1)} %last.1.own, bf16[64,2048]{1,0:T(8,128)(2,1)S(1)} %collective-permute-done.2.received), custom_call_target="tpu_custom_call" | custom-call | tf_op jit(solution)/shard_map/add/pallas_call | solution.py:268
  (8 shorter events, 0.0 us)
Async XLA Ops:
  0.0 4.5 %copy-start = (f32[2,48,128]{2,1,0:T(8,128)S(1)}, f32[2,48,128]{2,1,0:T(8,128)}, u32[]{:S(2)}) copy-start(f32[2,48,128]{2,1,0:T(8,128)} %level_angle.5) | copy-start | bytes 147460
  0.0 4.5 %copy-start.5 = (f32[48,64]{1,0:T(8,128)S(1)}, f32[48,64]{1,0:T(8,128)}, u32[]{:S(2)}) copy-start(f32[48,64]{1,0:T(8,128)} %lagrange.1) | copy-start | bytes 36868
  0.0 4.5 %copy-start.1 = (f32[2,96,96]{2,1,0:T(8,128)S(1)}, f32[2,96,96]{2,1,0:T(8,128)}, u32[]{:S(2)}) copy-start(f32[2,96,96]{2,1,0:T(8,128)} %level_self.3) | copy-start | bytes 221188
  0.0 4.5 %copy-start.2 = (f32[2,96,96]{2,1,0:T(8,128)S(1)}, f32[2,96,96]{2,1,0:T(8,128)}, u32[]{:S(2)}) copy-start(f32[2,96,96]{2,1,0:T(8,128)} %level_peer.3) | copy-start | bytes 221188
  1.2 10.6 %collective-permute-start = (bf16[18,64,128]{2,1,0:T(8,128)(2,1)S(1)}, bf16[18,64,128]{2,1,0:T(8,128)(2,1)S(1)}, u32[]{:S(2)}, u32[]{:S(2)}) collective-permute-start(bf16[18,64,128]{2,1,0:T(8,128)(2,1)S(1)} %get-tuple-element.17), channel_id=1, source_target_pairs={{0,1},{1,0},{2,3},{3,2},{4,5},{5,4},{6,7},{7,6},{8,9},{9,8},{10,11... | collective-permute-start | bytes 884744 | tf_op jit(solution)/shard_map/ppermute | solution.py:281
  13.5 18.7 %copy-start.7 = (f32[64,48]{0,1:T(8,128)S(1)}, f32[64,48]{0,1:T(8,128)}, u32[]{:S(2)}) copy-start(f32[64,48]{0,1:T(8,128)} %param.19) | copy-start | bytes 36868
  13.5 24.9 %copy-start.4 = (f32[96,96]{1,0:T(8,128)S(1)}, f32[96,96]{1,0:T(8,128)}, u32[]{:S(2)}) copy-start(f32[96,96]{1,0:T(8,128)} %switch_matrix.1) | copy-start | bytes 110596
  13.5 28.8 %all-to-all-start = ((bf16[64,24,128]{2,1,0:T(8,128)(2,1)}), bf16[64,24,128]{2,1,0:T(8,128)(2,1)S(1)}, u32[]{:S(2)}, u32[]{:S(2)}) async-start(bf16[64,24,128]{2,1,0:T(8,128)(2,1)} %bitcast), calls=%async_computation | async-start | bytes 786432 | tf_op jit(solution)/shard_map/all_to_all | solution.py:316
  27.4 10.9 %copy-start.3 = (f32[64,128]{1,0:T(8,128)S(1)}, f32[64,128]{1,0:T(8,128)}, u32[]{:S(2)}) copy-start(f32[64,128]{1,0:T(8,128)} %out_angle.3) | copy-start | bytes 98308
  27.4 10.9 %copy-start.6 = (f32[48,128]{1,0:T(8,128)S(1)}, f32[48,128]{1,0:T(8,128)}, u32[]{:S(2)}) copy-start(f32[48,128]{1,0:T(8,128)} %switch_angle.1) | copy-start | bytes 73732
  27.5 10.9 %collective-permute-start.1 = (f32[112,128]{1,0:T(8,128)S(1)}, f32[112,128]{1,0:T(8,128)S(1)}, u32[]{:S(2)}, u32[]{:S(2)}) collective-permute-start(f32[112,128]{1,0:T(8,128)S(1)} %get-tuple-element.23), channel_id=1, source_target_pairs={{0,4},{1,5},{2,6},{3,7},{4,0},{5,1},{6,2},{7,3},{8,12},{9,13},{10,... | collective-permute-start | bytes 172040 | tf_op jit(solution)/shard_map/ppermute | solution.py:281
  43.9 19.9 %collective-permute-start.2 = (bf16[64,2048]{1,0:T(8,128)(2,1)S(1)}, bf16[64,2048]{1,0:T(8,128)(2,1)S(1)}, u32[]{:S(2)}, u32[]{:S(2)}) collective-permute-start(bf16[64,2048]{1,0:T(8,128)(2,1)S(1)} %get-tuple-element.28), channel_id=1, source_target_pairs={{0,4},{1,5},{2,6},{3,7},{4,0},{5,1},{6,2},{7,3},{8,12},{9,13},{10,... | collective-permute-start | bytes 786440 | tf_op jit(solution)/shard_map/ppermute | solution.py:281

commit v4 on v3

--- a/solution.py
+++ b/solution.py
@@ -9,7 +9,7 @@
 BF16 = jnp.bfloat16
 LANES = 128
 CHUNK = 1024
-WHOLE = 2048
+WHOLE = 1024
 
 
 def sin_cos(angle):
@@ -53,17 +53,13 @@
     )
 
 
-def tall_weights(matrix):
-    return jnp.concatenate(halves(matrix), axis=0)
-
-
-def dot_exact(value, weights):
-    return dot(jnp.concatenate([value, value], axis=1), weights)
+def side_by_side(left, right, weights):
+    both = dot(jnp.concatenate([left, right], axis=1), weights)
+    return both[:, :LANES] + both[:, LANES:]
 
 
 def dot_wide(value, weights):
-    both = dot(jnp.concatenate(halves(value), axis=1), weights)
-    return both[:, :LANES] + both[:, LANES:]
+    return side_by_side(*halves(value), weights)
 
 
 def dot_full(left, right, dims=((1,), (0,))):
@@ -106,25 +102,20 @@
     return per_box(value, cos_factor) + per_box(pltpu.roll(value, 64, 1), sin_factor)
 
 
-def pack_kernel(charges, leaf_angle, level_angle, out_angle, out, held, angle, far_angle, sems):
+def pack_kernel(charges, leaf_angle, out, held, angle, sems):
     width = 512
     copies = []
     for step in range(2048 // width):
         here = pl.ds(step * width, width)
         copies.append(pltpu.make_async_copy(charges.at[:, here], held.at[:, here], sems.at[step]))
-    rest = [
-        pltpu.make_async_copy(leaf_angle, angle, sems.at[4]),
-        pltpu.make_async_copy(level_angle.at[1], far_angle.at[0:48], sems.at[5]),
-        pltpu.make_async_copy(out_angle, far_angle.at[48:112], sems.at[6]),
-    ]
-    for copy in copies + rest:
+    last = pltpu.make_async_copy(leaf_angle, angle, sems.at[4])
+    for copy in copies + [last]:
         copy.start()
     for step, copy in enumerate(copies):
         copy.wait()
         for tile in range(step * width // LANES, (step + 1) * width // LANES):
             out[tile] = held[:, tile * LANES : (tile + 1) * LANES].astype(BF16)
-    for copy in rest:
-        copy.wait()
+    last.wait()
     high, low = halves(angle[...])
     out[16] = high
     out[17] = low
@@ -185,90 +176,75 @@
             )
             for i, shift in enumerate((48, 32, 16))
         ]
-        packed = jnp.concatenate(packed, axis=1).reshape(CHUNK * 3 // 4, LANES)
-        out[chunk * CHUNK * 3 // 4 : (chunk + 1) * CHUNK * 3 // 4, :] = packed.astype(BF16)
+        packed = jnp.concatenate(packed * 2, axis=1).reshape(CHUNK * 3 // 2, LANES)
+        out[chunk * CHUNK * 3 // 2 : (chunk + 1) * CHUNK * 3 // 2, :] = packed.astype(BF16)
 
     source_part(lambda tile: received[tile].astype(F32), turned, weights[...], emit)
 
 
 def target_kernel(
-    level_angle, peer_angle, switch_angle, out_angle, level_self, level_peer, switch_matrix, evaluate, tall, wide, factors, scratch
+    side, level_angle, far_angle, switch_angle, out_angle, level_self, level_peer, switch_matrix, evaluate, switch_weights, level_weights, last_weights, factors, scratch
 ):
-    tall[0] = tall_weights(spread(switch_matrix, scratch).T)
-    tall[1] = tall_weights(spread(level_peer.at[1], scratch).T)
-    wide[0] = wide_weights(spread(level_self.at[1], scratch).T)
+    first = side[0] == 0
+    high, low = halves(spread(switch_matrix, scratch).T)
+    switch_weights[...] = jnp.concatenate([high, low], axis=0)
+    peer_matrix = spread(level_peer.at[1], scratch).T
+    self_matrix = spread(level_self.at[1], scratch).T
+    for place, matrix in enumerate((jnp.where(first, self_matrix, peer_matrix), jnp.where(first, peer_matrix, self_matrix))):
+        high, low = halves(matrix)
+        level_weights[place * LANES : (place + 1) * LANES, :] = jnp.concatenate([high, low], axis=1)
     scratch[...] = jnp.zeros((LANES, LANES), F32)
     scratch[0:64, 0:48] = evaluate[...]
     scratch[64:128, 64:112] = evaluate[...]
-    wide[1] = wide_weights(scratch[...].T)
-    factors[0], factors[1] = rotation_factors(switch_angle[...])
-    factors[2], factors[3] = rotation_factors(level_angle[1])
+    last_weights[...] = wide_weights(scratch[...].T)
+    here, there = switch_angle[...], far_angle[...]
+    factors[0], factors[1] = rotation_factors(jnp.where(first, here, there))
+    factors[2], factors[3] = rotation_factors(jnp.where(first, there, here))
+    factors[4], factors[5] = rotation_factors(level_angle[1])
     sine, cosine = sin_cos(out_angle[...])
-    factors[4] = jnp.concatenate([cosine, -sine], axis=0).T
-    factors[5], factors[6] = rotation_factors(peer_angle[0:48])
-    sine, cosine = sin_cos(peer_angle[48:112])
-    factors[7] = jnp.concatenate([cosine, -sine], axis=0).T
-
-
-def evaluated(value, cos_factor, sin_factor, out_factor, last_weights):
-    value = rotated(value, cos_factor, sin_factor)
-    value = dot_wide(value, last_weights)
-    value = per_box(value, out_factor)
-    tiles = []
-    for tile in range(value.shape[0] // LANES):
-        turned = value[tile * LANES : (tile + 1) * LANES, :].T
-        tiles.append(turned[0:64] + turned[64:128])
-    return jnp.concatenate(tiles, axis=1)
-
-
-def switch_kernel(received, tall, wide, factors, middle, sent):
+    factors[6] = jnp.concatenate([cosine, -sine], axis=0).T
+
+
+def field_kernel(received, switch_weights, level_weights, last_weights, factors, out):
     lane = lax.broadcasted_iota(jnp.int32, (WHOLE // 4, LANES), 1) % 64
     boxes = WHOLE // 16
     for chunk in range(2048 // WHOLE):
-        packed = received[chunk * WHOLE * 3 // 4 : (chunk + 1) * WHOLE * 3 // 4, :].astype(F32)
-        parts = packed.reshape(WHOLE // 32, 3, 8, LANES)
-        first = [parts[:, i].reshape(WHOLE // 4, LANES) for i in range(3)]
-        last = jnp.where(
-            lane < 16,
-            pltpu.roll(first[0], 80, 1),
-            jnp.where(lane < 32, pltpu.roll(first[1], 96, 1), pltpu.roll(first[2], 112, 1)),
-        )
-        value = jnp.concatenate(
-            [part.reshape(WHOLE // 32, 1, 8, LANES) for part in first + [last]], axis=1
-        ).reshape(WHOLE, LANES)
-        value = value.astype(BF16)
-        value = dot_exact(value, tall[0])
         here = pl.ds(chunk * boxes, boxes)
-        value = rotated(value, factors[0, here, :], factors[1, here, :])
-        middle[chunk * WHOLE : (chunk + 1) * WHOLE, :] = value
-        value = value.astype(BF16)
-        value = dot_exact(value, tall[1])
-        value = evaluated(value, factors[5, here, :], factors[6, here, :], factors[7, here, :], wide[1])
-        sent[:, chunk * WHOLE : (chunk + 1) * WHOLE] = value.astype(BF16)
-
-
-def last_kernel(middle, wide, factors, own):
-    boxes = CHUNK // 16
-    for chunk in range(2048 // CHUNK):
-        value = dot_wide(middle[chunk * CHUNK : (chunk + 1) * CHUNK, :], wide[0])
-        here = pl.ds(chunk * boxes, boxes)
-        own[:, chunk * CHUNK : (chunk + 1) * CHUNK] = evaluated(
-            value, factors[2, here, :], factors[3, here, :], factors[4, here, :], wide[1]
-        )
-
-
-def add_kernel(own, received, out):
-    out[...] = (own[...] + received[...].astype(F32)).astype(BF16)
-
-
-def call(kernel, outs, args, scratch=(), name=None, hbm=False):
+        packed = received[chunk * WHOLE * 3 // 2 : (chunk + 1) * WHOLE * 3 // 2, :].astype(F32)
+        parts = packed.reshape(WHOLE // 32, 6, 8, LANES)
+        sides = []
+        for side in range(2):
+            first = [parts[:, 3 * side + i].reshape(WHOLE // 4, LANES) for i in range(3)]
+            last = jnp.where(
+                lane < 16,
+                pltpu.roll(first[0], 80, 1),
+                jnp.where(lane < 32, pltpu.roll(first[1], 96, 1), pltpu.roll(first[2], 112, 1)),
+            )
+            value = jnp.concatenate(
+                [part.reshape(WHOLE // 32, 1, 8, LANES) for part in first + [last]], axis=1
+            ).reshape(WHOLE, LANES)
+            value = value.astype(BF16)
+            value = dot(jnp.concatenate([value, value], axis=1), switch_weights[...])
+            value = rotated(value, factors[2 * side, here, :], factors[2 * side + 1, here, :])
+            sides.append(value.astype(BF16))
+        value = side_by_side(*sides, level_weights[...])
+        value = rotated(value, factors[4, here, :], factors[5, here, :])
+        value = per_box(dot_wide(value, last_weights[...]), factors[6, here, :])
+        for tile in range(WHOLE // LANES):
+            turned = value[tile * LANES : (tile + 1) * LANES, :].T
+            at = chunk * WHOLE + tile * LANES
+            out[:, at : at + LANES] = (turned[0:64] + turned[64:128]).astype(BF16)
+
+
+def call(kernel, outs, args, scratch=(), name=None, spaces=pltpu.VMEM):
     whole = pl.BlockSpec(memory_space=pltpu.VMEM)
-    source = pl.BlockSpec(memory_space=pltpu.HBM) if hbm else whole
+    if not isinstance(spaces, list):
+        spaces = [spaces] * len(args)
     shapes = [jax.ShapeDtypeStruct(shape, dtype) for shape, dtype in outs]
     return pl.pallas_call(
         kernel,
         out_shape=shapes if len(shapes) > 1 else shapes[0],
-        in_specs=[source] * len(args),
+        in_specs=[pl.BlockSpec(memory_space=space) for space in spaces],
         out_specs=[whole] * len(shapes) if len(shapes) > 1 else whole,
         scratch_shapes=scratch,
         compiler_params=pltpu.CompilerParams(vmem_limit_bytes=32 * 1024 * 1024),
@@ -295,16 +271,17 @@
 ):
     square = (LANES, LANES)
     tile = pltpu.VMEM(square, F32)
-    packed, charges, leaf_angle, far_angle = call(
+    wide, narrow = lax.axis_size("wide"), lax.axis_size("narrow")
+    apart = narrow // 2
+    packed, charges, leaf_angle = call(
         pack_kernel,
-        [((18, 64, LANES), BF16), ((64, 2048), F32), ((64, LANES), F32), ((112, LANES), F32)],
-        [pltpu.with_memory_space_constraint(x, pltpu.HBM) for x in (charges, leaf_angle, level_angle, out_angle)],
-        [pltpu.SemaphoreType.DMA((7,))],
+        [((18, 64, LANES), BF16), ((64, 2048), F32), ((64, LANES), F32)],
+        [pltpu.with_memory_space_constraint(x, pltpu.HBM) for x in (charges, leaf_angle)],
+        [pltpu.SemaphoreType.DMA((5,))],
         name="pack",
-        hbm=True,
+        spaces=pltpu.HBM,
     )
     near = from_partner(packed, 1)
-    far_angle = from_partner(far_angle, 4)
     own, weights, factors = call(
         own_kernel,
         [((2048, LANES), F32), ((2 * LANES, 2 * LANES), BF16), ((2, *square), F32)],
@@ -312,24 +289,29 @@
         [tile] * 2,
         name="own",
     )
-    state = call(peer_kernel, [((1536, LANES), BF16)], [near, own, weights, factors], [tile], name="peer")
-    state = lax.all_to_all(state.reshape(64, 24, LANES), "wide", 0, 0, tiled=True).reshape(1536, LANES)
-    tall, wide, factors = call(
+    state = call(peer_kernel, [((3072, LANES), BF16)], [near, own, weights, factors], [tile], name="peer")
+    groups = [
+        [w * narrow + r + apart * side for w in range(wide) for side in range(2)] for r in range(apart)
+    ]
+    state = lax.all_to_all(
+        state.reshape(2 * wide, 24, LANES),
+        ("wide", "narrow"),
+        0,
+        0,
+        axis_index_groups=groups,
+        tiled=True,
+    ).reshape(3072, LANES)
+    far_angle = from_partner(switch_angle, apart)
+    side = (lax.axis_index("narrow") // apart).astype(jnp.int32).reshape(1)
+    *weights, factors = call(
         target_kernel,
-        [((2, 2 * LANES, LANES), BF16), ((2, 2 * LANES, 2 * LANES), BF16), ((8, *square), F32)],
-        [level_angle, far_angle, switch_angle, out_angle, level_self, level_peer, switch_matrix, evaluate],
+        [((2 * LANES, LANES), BF16), ((2 * LANES, 2 * LANES), BF16), ((2 * LANES, 2 * LANES), BF16), ((7, *square), F32)],
+        [side, level_angle, far_angle, switch_angle, out_angle, level_self, level_peer, switch_matrix, evaluate],
         [tile],
         name="target",
-    )
-    middle, sent = call(
-        switch_kernel,
-        [((2048, LANES), F32), ((64, 2048), BF16)],
-        [state, tall, wide, factors],
-        name="switch",
-    )
-    far = from_partner(sent, 4)
-    own = call(last_kernel, [((64, 2048), F32)], [middle, wide, factors], name="last")
-    return call(add_kernel, [((64, 2048), BF16)], [own, far], name="add")
+        spaces=[pltpu.SMEM] + [pltpu.VMEM] * 8,
+    )
+    return call(field_kernel, [((64, 2048), BF16)], [state, *weights, factors], name="field")
 
 
 def solution(mesh):

time: 65 us -> 65.6 us (level)
  the two profiles are of different devices: /device:TPU:56 before, /device:TPU:9 now
where the time goes in v4:
time: 65.6 us; the launch traced here: 65.3 us
  starting transfers between devices  31.6 us (48%)
  waiting for transfers between devices  26.6 us (41%)
  Pallas kernels  6.81 us (10%)
    all_to_all x1, starting transfers between devices, body(): lax.all_to_all(state.reshape(2 * wide, 24, LANES), ('wide', 'narrow'), 0,...  22.4 us
    ppermute x2, waiting for transfers between devices, from_partner(): return lax.ppermute(value, 'narrow', pairs)  20.6 us
    ppermute x2, starting transfers between devices, from_partner(): return lax.ppermute(value, 'narrow', pairs)  9.25 us
    pallas_call x5, Pallas kernels, call(): pl.pallas_call(kernel, out_shape=shapes if len(shapes) > 1 else shapes[0]...  6.81 us
    all_to_all x1, waiting for transfers between devices, body(): lax.all_to_all(state.reshape(2 * wide, 24, LANES), ('wide', 'narrow'), 0,...  5.97 us
  transfers between devices with their start and end apart: 3, of which 3 were waited for; matrix products, arithmetic and copies ran while one was open for 0% of the time, Pallas kernels for 2%

profile of v4, /device:TPU:9, one launch (start us, length us, event | category | flops | bytes accessed | tf_op | source)
XLA Modules:
  0.0 65.3 jit_solution(5595358935435892029)
XLA Ops:
  0.0 0.0 copy-start.5
  0.0 0.0 copy-start.1
  0.0 1.2 %pack.1 = (bf16[18,64,128]{2,1,0:T(8,128)(2,1)S(1)}, f32[64,2048]{1,0:T(8,128)S(1)}, f32[64,128]{1,0:T(8,128)S(1)}) custom-call(f32[64,2048]{1,0:T(8,128)} %charges.1, f32[64,128]{1,0:T(8,128)} %leaf_angle.1), custom_call_target="tpu_custom_call" | custom-call | tf_op jit(solution)/shard_map/pack/pallas_call | solution.py:244
  1.2 1.9 %collective-permute-start = (bf16[18,64,128]{2,1,0:T(8,128)(2,1)S(1)}, bf16[18,64,128]{2,1,0:T(8,128)(2,1)S(1)}, u32[]{:S(2)}, u32[]{:S(2)}) collective-permute-start(bf16[18,64,128]{2,1,0:T(8,128)(2,1)S(1)} %get-tuple-element.15), channel_id=1, source_target_pairs={{0,1},{1,0},{2,3},{3,2},{4,5},{5,4},{6,7},{7,6},{8,9},{9,8},{10,11... | collective-permute-start | bytes 884744 | tf_op jit(solution)/shard_map/ppermute | solution.py:257
  3.2 0.0 copy-done.5
  3.2 0.0 copy-done.2
  3.2 0.0 copy-done
  3.2 0.0 copy-done.1
  3.2 0.9 %own.1 = (f32[2048,128]{1,0:T(8,128)S(1)}, bf16[256,256]{1,0:T(8,128)(2,1)S(1)}, f32[2,128,128]{2,1,0:T(8,128)S(1)}) custom-call(f32[64,2048]{1,0:T(8,128)S(1)} %get-tuple-element.16.charges, f32[64,128]{1,0:T(8,128)S(1)} %get-tuple-element.17.leaf_angle, f32[48,64]{1,0:T(8,128)S(1)} %copy-done.5, f32[2,48,128]{2,1,0:T(8,128)S(1)} %copy-done.2, ...), custom_call_target="tpu_custom_call" | custom-call | tf_op jit(solution)/shard_map/own/pallas_call | solution.py:244
  4.1 4.6 %collective-permute-done.received = bf16[18,64,128]{2,1,0:T(8,128)(2,1)S(1)} collective-permute-done((bf16[18,64,128]{2,1,0:T(8,128)(2,1)S(1)}, bf16[18,64,128]{2,1,0:T(8,128)(2,1)S(1)}, u32[]{:S(2)}, u32[]{:S(2)}) %collective-permute-start) | collective-permute-done | bytes 294944 | tf_op jit(solution)/shard_map/ppermute | solution.py:257
  8.8 1.8 %peer.1 = bf16[3072,128]{1,0:T(8,128)(2,1)} custom-call(bf16[18,64,128]{2,1,0:T(8,128)(2,1)S(1)} %collective-permute-done.received, f32[2048,128]{1,0:T(8,128)S(1)} %get-tuple-element.18.own, bf16[256,256]{1,0:T(8,128)(2,1)S(1)} %get-tuple-element.19.weights, f32[2,128,128]{2,1,0:T(8,128)S(1)} %get-tuple-element.20.factors), custom_call_target="tpu_custom_call" | custom-call | tf_op jit(solution)/shard_map/peer/pallas_call | solution.py:244
  10.5 22.4 %all-to-all-start = ((bf16[128,24,128]{2,1,0:T(8,128)(2,1)}), bf16[128,24,128]{2,1,0:T(8,128)(2,1)S(1)}, u32[]{:S(2)}, u32[]{:S(2)}) async-start(bf16[128,24,128]{2,1,0:T(8,128)(2,1)} %bitcast), calls=%async_computation | async-start | bytes 1572864 | tf_op jit(solution)/shard_map/all_to_all | solution.py:296
  32.9 0.0 copy-done.6
  32.9 0.0 copy-start.3
  32.9 7.3 %collective-permute-start.1 = (f32[48,128]{1,0:T(8,128)S(1)}, f32[48,128]{1,0:T(8,128)S(1)}, u32[]{:S(2)}, u32[]{:S(2)}) collective-permute-start(f32[48,128]{1,0:T(8,128)S(1)} %copy-done.6), channel_id=1, source_target_pairs={{0,4},{1,5},{2,6},{3,7},{4,0},{5,1},{6,2},{7,3},{8,12},{9,13},{10,... | collective-permute-start | bytes 73736 | tf_op jit(solution)/shard_map/ppermute | solution.py:257
  40.3 0.0 copy-done.7
  40.3 0.0 copy-start.4
  40.3 0.1 copy.11.evaluate
  40.4 16.0 %collective-permute-done.1.far_angle = f32[48,128]{1,0:T(8,128)S(1)} collective-permute-done((f32[48,128]{1,0:T(8,128)S(1)}, f32[48,128]{1,0:T(8,128)S(1)}, u32[]{:S(2)}, u32[]{:S(2)}) %collective-permute-start.1) | collective-permute-done | bytes 24608 | tf_op jit(solution)/shard_map/ppermute | solution.py:257
  56.4 0.0 copy-done.3
  56.4 0.0 copy-done.4
  56.4 0.4 target.1
  56.7 6.0 %all-to-all-done = bf16[128,24,128]{2,1,0:T(8,128)(2,1)S(1)} async-done(((bf16[128,24,128]{2,1,0:T(8,128)(2,1)}), bf16[128,24,128]{2,1,0:T(8,128)(2,1)S(1)}, u32[]{:S(2)}, u32[]{:S(2)}) %all-to-all-start) | async-done | bytes 786464 | tf_op jit(solution)/shard_map/all_to_all | solution.py:296
  62.7 2.6 %field.1 = bf16[64,2048]{1,0:T(8,128)(2,1)} custom-call(bf16[3072,128]{1,0:T(8,128)(2,1)S(1)} %bitcast.3, bf16[256,128]{1,0:T(8,128)(2,1)S(1)} %get-tuple-element.21.switch_weights, bf16[256,256]{1,0:T(8,128)(2,1)S(1)} %get-tuple-element.22.level_weights, bf16[256,256]{1,0:T(8,128)(2,1)S(1)} %get-tuple-element.23.last_weights, ...), custom_call_target="tpu_custom_call" | custom-call | tf_op jit(solution)/shard_map/field/pallas_call | solution.py:244
  (4 shorter events, 0.0 us)
Async XLA Ops:
  0.0 3.2 %copy-start.5 = (f32[48,64]{1,0:T(8,128)S(1)}, f32[48,64]{1,0:T(8,128)}, u32[]{:S(2)}) copy-start(f32[48,64]{1,0:T(8,128)} %lagrange.1) | copy-start | bytes 36868
  0.0 3.2 %copy-start.2 = (f32[2,48,128]{2,1,0:T(8,128)S(1)}, f32[2,48,128]{2,1,0:T(8,128)}, u32[]{:S(2)}) copy-start(f32[2,48,128]{2,1,0:T(8,128)} %level_angle.3) | copy-start | bytes 147460
  0.0 3.2 %copy-start = (f32[2,96,96]{2,1,0:T(8,128)S(1)}, f32[2,96,96]{2,1,0:T(8,128)}, u32[]{:S(2)}) copy-start(f32[2,96,96]{2,1,0:T(8,128)} %level_self.3) | copy-start | bytes 221188
  0.0 3.2 %copy-start.1 = (f32[2,96,96]{2,1,0:T(8,128)S(1)}, f32[2,96,96]{2,1,0:T(8,128)}, u32[]{:S(2)}) copy-start(f32[2,96,96]{2,1,0:T(8,128)} %level_peer.3) | copy-start | bytes 221188
  1.2 7.5 %collective-permute-start = (bf16[18,64,128]{2,1,0:T(8,128)(2,1)S(1)}, bf16[18,64,128]{2,1,0:T(8,128)(2,1)S(1)}, u32[]{:S(2)}, u32[]{:S(2)}) collective-permute-start(bf16[18,64,128]{2,1,0:T(8,128)(2,1)S(1)} %get-tuple-element.15), channel_id=1, source_target_pairs={{0,1},{1,0},{2,3},{3,2},{4,5},{5,4},{6,7},{7,6},{8,9},{9,8},{10,11... | collective-permute-start | bytes 884744 | tf_op jit(solution)/shard_map/ppermute | solution.py:257
  10.5 22.4 %copy-start.6 = (f32[48,128]{1,0:T(8,128)S(1)}, f32[48,128]{1,0:T(8,128)}, u32[]{:S(2)}) copy-start(f32[48,128]{1,0:T(8,128)} %switch_angle.1) | copy-start | bytes 73732
  10.5 29.8 %copy-start.7 = (f32[64,48]{0,1:T(8,128)S(1)}, f32[64,48]{0,1:T(8,128)}, u32[]{:S(2)}) copy-start(f32[64,48]{0,1:T(8,128)} %param.19) | copy-start | bytes 36868
  10.5 52.2 %all-to-all-start = ((bf16[128,24,128]{2,1,0:T(8,128)(2,1)}), bf16[128,24,128]{2,1,0:T(8,128)(2,1)S(1)}, u32[]{:S(2)}, u32[]{:S(2)}) async-start(bf16[128,24,128]{2,1,0:T(8,128)(2,1)} %bitcast), calls=%async_computation | async-start | bytes 1572864 | tf_op jit(solution)/shard_map/all_to_all | solution.py:296
  32.9 23.4 %copy-start.3 = (f32[96,96]{1,0:T(8,128)S(1)}, f32[96,96]{1,0:T(8,128)}, u32[]{:S(2)}) copy-start(f32[96,96]{1,0:T(8,128)} %switch_matrix.1) | copy-start | bytes 110596
  32.9 23.4 %collective-permute-start.1 = (f32[48,128]{1,0:T(8,128)S(1)}, f32[48,128]{1,0:T(8,128)S(1)}, u32[]{:S(2)}, u32[]{:S(2)}) collective-permute-start(f32[48,128]{1,0:T(8,128)S(1)} %copy-done.6), channel_id=1, source_target_pairs={{0,4},{1,5},{2,6},{3,7},{4,0},{5,1},{6,2},{7,3},{8,12},{9,13},{10,... | collective-permute-start | bytes 73736 | tf_op jit(solution)/shard_map/ppermute | solution.py:257
  40.3 16.1 %copy-start.4 = (f32[64,128]{1,0:T(8,128)S(1)}, f32[64,128]{1,0:T(8,128)}, u32[]{:S(2)}) copy-start(f32[64,128]{1,0:T(8,128)} %out_angle.1) | copy-start | bytes 98308

commit v5 on v3

v5 whole, which is shorter than its diff:
```python
import jax
import jax.numpy as jnp
from jax import lax
from jax.experimental import pallas as pl
from jax.experimental.pallas import tpu as pltpu
from jax.sharding import PartitionSpec as P

F32 = jnp.float32
BF16 = jnp.bfloat16
LANES = 128
CHUNK = 1024
WHOLE = 2048


def sin_cos(angle):
    turns = jnp.floor(angle * 0.6366197723675814 + 0.5)
    rest = angle - turns * 1.5703125
    rest = rest - turns * 4.837512969970703125e-4
    rest = rest - turns * 7.549789948768648e-8
    square = rest * rest
    sine = rest + rest * square * (
        -1.6666654611e-1 + square * (8.3321608736e-3 + square * -1.9515295891e-4)
    )
    cosine = (
        1.0
        - 0.5 * square
        + square
        * square
        * (4.166664568298827e-2 + square * (-1.388731625493765e-3 + square * 2.443315711809948e-5))
    )
    size = jnp.abs(turns)
    odd = size == 1.0
    sign = jnp.where(size == 2.0, -1.0, 1.0)
    return (
        jnp.where(odd, turns * cosine, sign * sine),
        jnp.where(odd, -turns * sine, sign * cosine),
    )


def halves(value):
    high = value.astype(BF16)
    return high, (value - high.astype(F32)).astype(BF16)


def dot(left, right):
    return jnp.dot(left, right, preferred_element_type=F32)


def wide_weights(matrix):
    high, low = halves(matrix)
    return jnp.concatenate(
        [jnp.concatenate([high, low], axis=1), jnp.concatenate([high, jnp.zeros_like(low)], axis=1)], axis=0
    )


def tall_weights(matrix):
    return jnp.concatenate(halves(matrix), axis=0)


def dot_exact(value, weights):
    return dot(jnp.concatenate([value, value], axis=1), weights)


def dot_wide(value, weights):
    both = dot(jnp.concatenate(halves(value), axis=1), weights)
    return both[:, :LANES] + both[:, LANES:]


def dot_full(left, right, dims=((1,), (0,))):
    return lax.dot_general(
        left, right, (dims, ((), ())), precision=lax.Precision.HIGHEST, preferred_element_type=F32
    )


def spread(rows, scratch):
    scratch[...] = jnp.zeros((LANES, LANES), F32)
    for to_row, from_row in ((0, 0), (64, 48)):
        for to_lane, from_lane in ((0, 0), (64, 48)):
            scratch[to_row : to_row + 48, to_lane : to_lane + 48] = rows[
                from_row : from_row + 48, from_lane : from_lane + 48
            ]
    return scratch[...]


def two_blocks(block, scratch):
    scratch[...] = jnp.zeros((LANES, LANES), F32)
    scratch[0:48, 0:64] = block
    scratch[64:112, 64:128] = block
    return scratch[...]


def rotation_factors(angle):
    sine, cosine = sin_cos(angle)
    gap = jnp.zeros((16, LANES), F32)
    cos_rows = jnp.concatenate([cosine, gap, cosine, gap], axis=0)
    sin_rows = jnp.concatenate([-sine, gap, sine, gap], axis=0)
    return cos_rows.T, sin_rows.T


def per_box(value, factor):
    boxes = factor.shape[0]
    return (value.reshape(boxes, 16, LANES) * factor[:, None, :]).reshape(boxes * 16, LANES)


def rotated(value, cos_factor, sin_factor):
    return per_box(value, cos_factor) + per_box(pltpu.roll(value, 64, 1), sin_factor)


GROUP = 4
PIECE = 20


def piece_rows(backward):
    pieces = lax.broadcasted_iota(jnp.int32, (8 * PIECE, 8 * PIECE), 1 if backward else 0)
    rows = lax.broadcasted_iota(jnp.int32, (8 * PIECE, 8 * PIECE), 0 if backward else 1)
    place, row = pieces // PIECE, pieces % PIECE
    wide, side = place // 2, place % 2
    angle = row - 16
    found = jnp.where(row < 16, wide * 16 + row, 64 + (angle // 2) * 8 + wide * 2 + angle % 2)
    if backward:
        return (rows == side * 80 + found).astype(F32).astype(BF16)
    return (rows == found).astype(F32).astype(BF16)[:, :80]


def angle_rows(angle):
    high = angle.astype(BF16).astype(F32)
    low = angle - high
    if angle.shape[0] == 64:
        return jnp.concatenate([high, low], axis=0).T
    gap = jnp.zeros((16, LANES), F32)
    return jnp.concatenate([high, gap, low, gap], axis=0).T


def pack_kernel(charges, leaf_angle, level_angle, out_angle, out, far_angle, held, angle, first_angle, sems):
    width = 512
    copies = []
    for step in range(2048 // width):
        here = pl.ds(step * width, width)
        copies.append(pltpu.make_async_copy(charges.at[:, here], held.at[:, here], sems.at[step]))
    near = [
        pltpu.make_async_copy(leaf_angle, angle, sems.at[4]),
        pltpu.make_async_copy(level_angle.at[0], first_angle, sems.at[5]),
    ]
    far = [
        pltpu.make_async_copy(level_angle.at[1], far_angle.at[0:48], sems.at[6]),
        pltpu.make_async_copy(out_angle, far_angle.at[48:112], sems.at[7]),
    ]
    for copy in near + copies + far:
        copy.start()
    order = piece_rows(False)
    low_lane = lax.broadcasted_iota(jnp.int32, (64, LANES), 1) < 64
    for copy in near:
        copy.wait()
    leaf_rows = angle_rows(angle[...])
    level_rows = angle_rows(first_angle[...])
    for tile in range(16):
        if tile % 4 == 0:
            copies[tile // 4].wait()
        points = held[:, tile * LANES : (tile + 1) * LANES]
        both = jnp.concatenate([points, points], axis=0).T.reshape(GROUP, 2, 16, LANES)
        merged = jnp.where(low_lane, both[:, 0].reshape(64, LANES), both[:, 1].reshape(64, LANES))
        boxes = slice(tile * 8, (tile + 1) * 8)
        rows = jnp.concatenate([merged, leaf_rows[boxes], level_rows[boxes]], axis=0).astype(BF16)
        out[tile * 160 : (tile + 1) * 160, :] = dot(order, rows).astype(BF16)
    for copy in far:
        copy.wait()


def target_kernel(
    parity, lagrange, level_angle, peer_angle, switch_angle, out_angle, level_self, level_peer, switch_matrix, evaluate, source, tall, wide, factors, scratch
):
    leaf = two_blocks(lagrange[...], scratch)
    self_weights = dot_full(leaf, spread(level_self.at[0], scratch), ((0,), (1,)))
    peer_weights = dot_full(leaf, spread(level_peer.at[0], scratch), ((0,), (1,)))
    even = parity[0] == 0
    for place in range(2):
        near, far = (self_weights, peer_weights) if place == 0 else (peer_weights, self_weights)
        high, low = halves(jnp.where(even, near, far))
        source[place * LANES : (place + 1) * LANES, :] = jnp.concatenate([high, low], axis=1)
    tall[...] = tall_weights(spread(level_peer.at[1], scratch).T)
    wide[0] = wide_weights(spread(level_self.at[1], scratch).T)
    scratch[...] = jnp.zeros((LANES, LANES), F32)
    scratch[0:64, 0:48] = evaluate[...]
    scratch[64:128, 64:112] = evaluate[...]
    wide[1] = wide_weights(scratch[...].T)
    wide[2] = wide_weights(spread(switch_matrix, scratch).T)
    factors[0], factors[1] = rotation_factors(switch_angle[...])
    factors[2], factors[3] = rotation_factors(level_angle[1])
    sine, cosine = sin_cos(out_angle[...])
    factors[4] = jnp.concatenate([cosine, -sine], axis=0).T
    factors[5], factors[6] = rotation_factors(peer_angle[0:48])
    sine, cosine = sin_cos(peer_angle[48:112])
    factors[7] = jnp.concatenate([cosine, -sine], axis=0).T


def evaluated(value, cos_factor, sin_factor, out_factor, last_weights):
    value = rotated(value, cos_factor, sin_factor)
    value = dot_wide(value, last_weights)
    value = per_box(value, out_factor)
    tiles = []
    for tile in range(value.shape[0] // LANES):
        turned = value[tile * LANES : (tile + 1) * LANES, :].T
        tiles.append(turned[0:64] + turned[64:128])
    return jnp.concatenate(tiles, axis=1)


def switch_kernel(parity, received, source, tall, wide, factors, middle, sent, points, turns):
    order = piece_rows(True)
    low_lane = lax.broadcasted_iota(jnp.int32, (64, LANES), 1) < 64
    for group in range(16):
        rows = dot(order, received[group * 160 : (group + 1) * 160, :])
        for side in range(2):
            merged = rows[side * 80 : side * 80 + 64]
            exchanged = pltpu.roll(merged, 64, 1)
            pair = [
                jnp.where(low_lane, merged, exchanged).reshape(GROUP, 1, 16, LANES),
                jnp.where(low_lane, exchanged, merged).reshape(GROUP, 1, 16, LANES),
            ]
            points[side, group * LANES : (group + 1) * LANES, :] = jnp.concatenate(pair, axis=1).reshape(LANES, LANES)
            turns[side, group * 8 : (group + 1) * 8, :] = rows[side * 80 + 64 : side * 80 + 72]
            turns[2 + side, group * 8 : (group + 1) * 8, :] = rows[side * 80 + 72 : side * 80 + 80]
    first_half = lax.broadcasted_iota(jnp.int32, (LANES, LANES), 1) < 64
    for side in range(2):
        angle = turns[side] + pltpu.roll(turns[side], 64, 1)
        sine, cosine = sin_cos(angle)
        turns[side] = jnp.where(first_half, cosine, sine)
    angle = jnp.where(parity[0] == 0, turns[2], turns[3])
    sine, cosine = sin_cos(angle + pltpu.roll(angle, 64, 1))
    turns[2] = cosine
    turns[3] = jnp.where(first_half, -sine, sine)
    boxes = WHOLE // 16
    for chunk in range(2048 // WHOLE):
        here = pl.ds(chunk * boxes, boxes)
        there = pl.ds(chunk * WHOLE, WHOLE)
        parts = [halves(per_box(points[side, there, :], turns[side, here, :])) for side in range(2)]
        both = dot(jnp.concatenate([parts[0][0], parts[1][0]], axis=1), source[...])
        value = both[:, :LANES] + both[:, LANES:]
        value = value + dot(jnp.concatenate([parts[0][1], parts[1][1]], axis=1), source[:, :LANES])
        value = rotated(value, turns[2, here, :], turns[3, here, :])
        value = dot_wide(value, wide[2])
        value = rotated(value, factors[0, here, :], factors[1, here, :])
        middle[there, :] = value
        value = dot_exact(value.astype(BF16), tall[...])
        value = evaluated(value, factors[5, here, :], factors[6, here, :], factors[7, here, :], wide[1])
        sent[:, there] = value.astype(BF16)


def last_kernel(middle, wide, factors, own):
    boxes = CHUNK // 16
    for chunk in range(2048 // CHUNK):
        value = dot_wide(middle[chunk * CHUNK : (chunk + 1) * CHUNK, :], wide[0])
        here = pl.ds(chunk * boxes, boxes)
        own[:, chunk * CHUNK : (chunk + 1) * CHUNK] = evaluated(
            value, factors[2, here, :], factors[3, here, :], factors[4, here, :], wide[1]
        )


def add_kernel(own, received, out):
    out[...] = (own[...] + received[...].astype(F32)).astype(BF16)


def call(kernel, outs, args, scratch=(), name=None, spaces=()):
    whole = pl.BlockSpec(memory_space=pltpu.VMEM)
    spaces = list(spaces) + [pltpu.VMEM] * (len(args) - len(spaces))
    shapes = [jax.ShapeDtypeStruct(shape, dtype) for shape, dtype in outs]
    return pl.pallas_call(
        kernel,
        out_shape=shapes if len(shapes) > 1 else shapes[0],
        in_specs=[pl.BlockSpec(memory_space=space) for space in spaces],
        out_specs=[whole] * len(shapes) if len(shapes) > 1 else whole,
        scratch_shapes=scratch,
        compiler_params=pltpu.CompilerParams(vmem_limit_bytes=32 * 1024 * 1024),
        name=name,
    )(*args)


def from_partner(value, apart):
    pairs = [(source, source ^ apart) for source in range(lax.axis_size("narrow"))]
    return lax.ppermute(value, "narrow", pairs)


def body(
    charges,
    leaf_angle,
    lagrange,
    level_angle,
    level_self,
    level_peer,
    switch_angle,
    switch_matrix,
    out_angle,
    evaluate,
):
    square = (LANES, LANES)
    tile = pltpu.VMEM(square, F32)
    wide, narrow = lax.axis_size("wide"), lax.axis_size("narrow")
    packed, far_angle = call(
        pack_kernel,
        [((128 * PIECE, LANES), BF16), ((112, LANES), F32)],
        [pltpu.with_memory_space_constraint(x, pltpu.HBM) for x in (charges, leaf_angle, level_angle, out_angle)],
        [
            pltpu.VMEM((64, 2048), F32),
            pltpu.VMEM((64, LANES), F32),
            pltpu.VMEM((48, LANES), F32),
            pltpu.SemaphoreType.DMA((8,)),
        ],
        name="pack",
        spaces=[pltpu.HBM] * 4,
    )
    groups = [[w * narrow + r + side for w in range(wide) for side in range(2)] for r in range(0, narrow, 2)]
    packed = lax.all_to_all(
        packed.reshape(2 * wide, PIECE // 4, 4, LANES),
        ("wide", "narrow"),
        0,
        0,
        axis_index_groups=groups,
        tiled=True,
    ).reshape(128 * PIECE, LANES)
    far_angle = from_partner(far_angle, narrow // 2)
    parity = (lax.axis_index("narrow") & 1).astype(jnp.int32).reshape(1)
    source, tall, both, factors = call(
        target_kernel,
        [
            ((2 * LANES, 2 * LANES), BF16),
            ((2 * LANES, LANES), BF16),
            ((3, 2 * LANES, 2 * LANES), BF16),
            ((8, *square), F32),
        ],
        [parity, lagrange, level_angle, far_angle, switch_angle, out_angle, level_self, level_peer, switch_matrix, evaluate],
        [tile],
        name="target",
        spaces=[pltpu.SMEM],
    )
    middle, sent = call(
        switch_kernel,
        [((2048, LANES), F32), ((64, 2048), BF16)],
        [parity, packed, source, tall, both, factors],
        [pltpu.VMEM((2, 2048, LANES), F32), pltpu.VMEM((4, *square), F32)],
        name="switch",
        spaces=[pltpu.SMEM],
    )
    far = from_partner(sent, narrow // 2)
    own = call(last_kernel, [((64, 2048), F32)], [middle, both, factors], name="last")
    return call(add_kernel, [((64, 2048), BF16)], [own, far], name="add")


def solution(mesh):
    return jax.shard_map(
        body,
        mesh=mesh,
        in_specs=(
            P(None, ("wide", "narrow")),
            P(None, ("wide", "narrow")),
            P(),
            P(None, None, ("wide", "narrow")),
            P(),
            P(),
            P(None, ("wide", "narrow")),
            P(),
            P(None, ("wide", "narrow")),
            P(),
        ),
        out_specs=P(None, ("wide", "narrow")),
        check_vma=False,
    )
```

time: 65 us -> 64.4 us (level)
  starting transfers between devices: 26.6 us -> 25.3 us
  Pallas kernels: 7.57 us -> 8.29 us
    ppermute x3 -> x2, waiting for transfers between devices: 26.6 us -> 20.1 us  [from_partner(): return lax.ppermute(value, 'narrow', pairs)]
    all_to_all x1, waiting for transfers between devices: 3.54 us -> 9.88 us  [body(): lax.all_to_all(packed.reshape(2 * wide, PIECE // 4, 4, LANES), ('wide', '...]
    ppermute x3 -> x2, starting transfers between devices: 12.7 us -> 9.54 us  [from_partner(): return lax.ppermute(value, 'narrow', pairs)]
    all_to_all x1, starting transfers between devices: 13.9 us -> 15.7 us  [body(): lax.all_to_all(packed.reshape(2 * wide, PIECE // 4, 4, LANES), ('wide', '...]
    pallas_call x7 -> x5, Pallas kernels: 7.57 us -> 8.29 us  [call(): pl.pallas_call(kernel, out_shape=shapes if len(shapes) > 1 else shapes[0]...]
  transfers between devices with their start and end apart: 4 -> 3, of which waited for: 4 -> 3; matrix products, arithmetic and copies ran while one was open for 0% -> 0% of each run, Pallas kernels for 4% -> 3%
where the time goes in v5:
time: 64.4 us; the launch traced here: 63.8 us
  waiting for transfers between devices  30 us (47%)
  starting transfers between devices  25.3 us (39%)
  Pallas kernels  8.29 us (13%)
    ppermute x2, waiting for transfers between devices, from_partner(): return lax.ppermute(value, 'narrow', pairs)  20.1 us
    all_to_all x1, starting transfers between devices, body(): lax.all_to_all(packed.reshape(2 * wide, PIECE // 4, 4, LANES), ('wide', '...  15.7 us
    all_to_all x1, waiting for transfers between devices, body(): lax.all_to_all(packed.reshape(2 * wide, PIECE // 4, 4, LANES), ('wide', '...  9.88 us
    ppermute x2, starting transfers between devices, from_partner(): return lax.ppermute(value, 'narrow', pairs)  9.54 us
    pallas_call x5, Pallas kernels, call(): pl.pallas_call(kernel, out_shape=shapes if len(shapes) > 1 else shapes[0]...  8.29 us
  transfers between devices with their start and end apart: 3, of which 3 were waited for; matrix products, arithmetic and copies ran while one was open for 0% of the time, Pallas kernels for 3%

profile of v5, /device:TPU:56, one launch (start us, length us, event | category | flops | bytes accessed | tf_op | source)
XLA Modules:
  0.0 63.8 jit_solution(17778795715684784421)
XLA Ops:
  0.0 3.0 %pack.1 = (bf16[2560,128]{1,0:T(8,128)(2,1)}, f32[112,128]{1,0:T(8,128)S(1)}) custom-call(f32[64,2048]{1,0:T(8,128)} %charges.1, f32[64,128]{1,0:T(8,128)} %leaf_angle.1, f32[2,48,128]{2,1,0:T(8,128)} %level_angle.3, f32[64,128]{1,0:T(8,128)} %out_angle.3), custom_call_target="tpu_custom_call" | custom-call | tf_op jit(solution)/shard_map/pack/pallas_call | solution.py:266
  3.0 0.0 copy-start.7
  3.0 0.0 copy-start.1
  3.0 0.0 copy-start.2
  3.0 0.0 copy-start.3
  3.0 0.0 copy-start.4
  3.0 0.0 copy-start.5
  3.0 0.0 copy-start.6
  3.0 15.7 %all-to-all-start = ((bf16[128,5,4,128]{3,2,1,0:T(4,128)(2,1)}), bf16[128,5,4,128]{3,2,1,0:T(4,128)(2,1)S(1)}, u32[]{:S(2)}, u32[]{:S(2)}) async-start(bf16[128,5,4,128]{3,2,1,0:T(4,128)(2,1)} %bitcast.1), calls=%async_computation | async-start | bytes 1310720 | tf_op jit(solution)/shard_map/all_to_all | solution.py:311
  18.8 0.0 copy-start
  18.8 4.8 %collective-permute-start = (f32[112,128]{1,0:T(8,128)S(1)}, f32[112,128]{1,0:T(8,128)S(1)}, u32[]{:S(2)}, u32[]{:S(2)}) collective-permute-start(f32[112,128]{1,0:T(8,128)S(1)} %get-tuple-element.14), channel_id=1, source_target_pairs={{0,4},{1,5},{2,6},{3,7},{4,0},{5,1},{6,2},{7,3},{8,12},{9,13},{10,... | collective-permute-start | bytes 172040 | tf_op jit(solution)/shard_map/ppermute | solution.py:279
  23.6 0.0 copy-done.7
  23.7 0.1 copy.11.evaluate
  23.7 6.4 %collective-permute-done.peer_angle = f32[112,128]{1,0:T(8,128)S(1)} collective-permute-done((f32[112,128]{1,0:T(8,128)S(1)}, f32[112,128]{1,0:T(8,128)S(1)}, u32[]{:S(2)}, u32[]{:S(2)}) %collective-permute-start) | collective-permute-done | bytes 57376 | tf_op jit(solution)/shard_map/ppermute | solution.py:279
  30.2 0.0 copy-done.1
  30.2 0.0 copy-done.2
  30.2 0.0 copy-done.3
  30.2 0.6 target.1
  30.8 9.9 %all-to-all-done = bf16[128,5,4,128]{3,2,1,0:T(4,128)(2,1)S(1)} async-done(((bf16[128,5,4,128]{3,2,1,0:T(4,128)(2,1)}), bf16[128,5,4,128]{3,2,1,0:T(4,128)(2,1)S(1)}, u32[]{:S(2)}, u32[]{:S(2)}) %all-to-all-start) | async-done | bytes 655392 | tf_op jit(solution)/shard_map/all_to_all | solution.py:311
  40.7 2.9 %switch.1 = (f32[2048,128]{1,0:T(8,128)S(1)}, bf16[64,2048]{1,0:T(8,128)(2,1)S(1)}) custom-call(s32[1]{0:T(128)} %bitcast.parity, bf16[2560,128]{1,0:T(8,128)(2,1)S(1)} %bitcast.3, bf16[256,256]{1,0:T(8,128)(2,1)S(1)} %get-tuple-element.15.source, bf16[256,128]{1,0:T(8,128)(2,1)S(1)} %get-tuple-element.16.tall, ...), custom_call_target="tpu_custom_call" | custom-call | tf_op jit(solution)/shard_map/switch/pallas_call | solution.py:266
  43.6 4.7 %collective-permute-start.1 = (bf16[64,2048]{1,0:T(8,128)(2,1)S(1)}, bf16[64,2048]{1,0:T(8,128)(2,1)S(1)}, u32[]{:S(2)}, u32[]{:S(2)}) collective-permute-start(bf16[64,2048]{1,0:T(8,128)(2,1)S(1)} %get-tuple-element.20), channel_id=1, source_target_pairs={{0,4},{1,5},{2,6},{3,7},{4,0},{5,1},{6,2},{7,3},{8,12},{9,13},{10,... | collective-permute-start | bytes 786440 | tf_op jit(solution)/shard_map/ppermute | solution.py:279
  48.3 1.1 %last.1.own = f32[64,2048]{1,0:T(8,128)S(1)} custom-call(f32[2048,128]{1,0:T(8,128)S(1)} %get-tuple-element.19.middle, bf16[3,256,256]{2,1,0:T(8,128)(2,1)S(1)} %get-tuple-element.17.wide, f32[8,128,128]{2,1,0:T(8,128)S(1)} %get-tuple-element.18.factors), custom_call_target="tpu_custom_call" | custom-call | tf_op jit(solution)/shard_map/last/pallas_call | solution.py:266
  49.4 13.7 %collective-permute-done.1.received = bf16[64,2048]{1,0:T(8,128)(2,1)S(1)} collective-permute-done((bf16[64,2048]{1,0:T(8,128)(2,1)S(1)}, bf16[64,2048]{1,0:T(8,128)(2,1)S(1)}, u32[]{:S(2)}, u32[]{:S(2)}) %collective-permute-start.1) | collective-permute-done | bytes 262176 | tf_op jit(solution)/shard_map/ppermute | solution.py:279
  63.1 0.8 %add.1 = bf16[64,2048]{1,0:T(8,128)(2,1)} custom-call(f32[64,2048]{1,0:T(8,128)S(1)} %last.1.own, bf16[64,2048]{1,0:T(8,128)(2,1)S(1)} %collective-permute-done.1.received), custom_call_target="tpu_custom_call" | custom-call | tf_op jit(solution)/shard_map/add/pallas_call | solution.py:266
  (4 shorter events, 0.0 us)
Async XLA Ops:
  3.0 20.7 %copy-start.7 = (f32[64,48]{0,1:T(8,128)S(1)}, f32[64,48]{0,1:T(8,128)}, u32[]{:S(2)}) copy-start(f32[64,48]{0,1:T(8,128)} %param.19) | copy-start | bytes 36868
  3.0 27.2 %copy-start.1 = (f32[64,128]{1,0:T(8,128)S(1)}, f32[64,128]{1,0:T(8,128)}, u32[]{:S(2)}) copy-start(f32[64,128]{1,0:T(8,128)} %out_angle.3) | copy-start | bytes 98308
  3.0 27.2 %copy-start.2 = (f32[2,96,96]{2,1,0:T(8,128)S(1)}, f32[2,96,96]{2,1,0:T(8,128)}, u32[]{:S(2)}) copy-start(f32[2,96,96]{2,1,0:T(8,128)} %level_self.1) | copy-start | bytes 221188
  3.0 27.2 %copy-start.3 = (f32[2,96,96]{2,1,0:T(8,128)S(1)}, f32[2,96,96]{2,1,0:T(8,128)}, u32[]{:S(2)}) copy-start(f32[2,96,96]{2,1,0:T(8,128)} %level_peer.1) | copy-start | bytes 221188
  3.0 27.2 %copy-start.4 = (f32[96,96]{1,0:T(8,128)S(1)}, f32[96,96]{1,0:T(8,128)}, u32[]{:S(2)}) copy-start(f32[96,96]{1,0:T(8,128)} %switch_matrix.1) | copy-start | bytes 110596
  3.0 27.2 %copy-start.5 = (f32[48,64]{1,0:T(8,128)S(1)}, f32[48,64]{1,0:T(8,128)}, u32[]{:S(2)}) copy-start(f32[48,64]{1,0:T(8,128)} %lagrange.1) | copy-start | bytes 36868
  3.0 27.2 %copy-start.6 = (f32[48,128]{1,0:T(8,128)S(1)}, f32[48,128]{1,0:T(8,128)}, u32[]{:S(2)}) copy-start(f32[48,128]{1,0:T(8,128)} %switch_angle.1) | copy-start | bytes 73732
  3.0 37.6 %all-to-all-start = ((bf16[128,5,4,128]{3,2,1,0:T(4,128)(2,1)}), bf16[128,5,4,128]{3,2,1,0:T(4,128)(2,1)S(1)}, u32[]{:S(2)}, u32[]{:S(2)}) async-start(bf16[128,5,4,128]{3,2,1,0:T(4,128)(2,1)} %bitcast.1), calls=%async_computation | async-start | bytes 1310720 | tf_op jit(solution)/shard_map/all_to_all | solution.py:311
  18.8 11.4 %copy-start = (f32[2,48,128]{2,1,0:T(8,128)S(1)}, f32[2,48,128]{2,1,0:T(8,128)}, u32[]{:S(2)}) copy-start(f32[2,48,128]{2,1,0:T(8,128)} %level_angle.3) | copy-start | bytes 147460
  18.8 11.4 %collective-permute-start = (f32[112,128]{1,0:T(8,128)S(1)}, f32[112,128]{1,0:T(8,128)S(1)}, u32[]{:S(2)}, u32[]{:S(2)}) collective-permute-start(f32[112,128]{1,0:T(8,128)S(1)} %get-tuple-element.14), channel_id=1, source_target_pairs={{0,4},{1,5},{2,6},{3,7},{4,0},{5,1},{6,2},{7,3},{8,12},{9,13},{10,... | collective-permute-start | bytes 172040 | tf_op jit(solution)/shard_map/ppermute | solution.py:279
  43.6 19.5 %collective-permute-start.1 = (bf16[64,2048]{1,0:T(8,128)(2,1)S(1)}, bf16[64,2048]{1,0:T(8,128)(2,1)S(1)}, u32[]{:S(2)}, u32[]{:S(2)}) collective-permute-start(bf16[64,2048]{1,0:T(8,128)(2,1)S(1)} %get-tuple-element.20), channel_id=1, source_target_pairs={{0,4},{1,5},{2,6},{3,7},{4,0},{5,1},{6,2},{7,3},{8,12},{9,13},{10,... | collective-permute-start | bytes 786440 | tf_op jit(solution)/shard_map/ppermute | solution.py:279

commit v6 on v5

--- a/solution.py
+++ b/solution.py
@@ -149,21 +149,21 @@
         copy.start()
     order = piece_rows(False)
     low_lane = lax.broadcasted_iota(jnp.int32, (64, LANES), 1) < 64
-    for copy in near:
+    for copy in near + copies + far:
         copy.wait()
     leaf_rows = angle_rows(angle[...])
     level_rows = angle_rows(first_angle[...])
-    for tile in range(16):
-        if tile % 4 == 0:
-            copies[tile // 4].wait()
-        points = held[:, tile * LANES : (tile + 1) * LANES]
-        both = jnp.concatenate([points, points], axis=0).T.reshape(GROUP, 2, 16, LANES)
-        merged = jnp.where(low_lane, both[:, 0].reshape(64, LANES), both[:, 1].reshape(64, LANES))
-        boxes = slice(tile * 8, (tile + 1) * 8)
-        rows = jnp.concatenate([merged, leaf_rows[boxes], level_rows[boxes]], axis=0).astype(BF16)
-        out[tile * 160 : (tile + 1) * 160, :] = dot(order, rows).astype(BF16)
-    for copy in far:
-        copy.wait()
+    for pair in range(8):
+        rows = []
+        for tile in (2 * pair, 2 * pair + 1):
+            points = held[:, tile * LANES : (tile + 1) * LANES]
+            both = jnp.concatenate([points, points], axis=0).T.reshape(GROUP, 2, 16, LANES)
+            merged = jnp.where(low_lane, both[:, 0].reshape(64, LANES), both[:, 1].reshape(64, LANES))
+            boxes = slice(tile * 8, (tile + 1) * 8)
+            rows.append(jnp.concatenate([merged, leaf_rows[boxes], level_rows[boxes]], axis=0).astype(BF16))
+        rows = dot(order, jnp.concatenate(rows, axis=1)).astype(BF16)
+        out[pair * 320 : pair * 320 + 160, :] = rows[:, :LANES]
+        out[pair * 320 + 160 : pair * 320 + 320, :] = rows[:, LANES:]
 
 
 def target_kernel(
@@ -208,15 +208,17 @@
     order = piece_rows(True)
     low_lane = lax.broadcasted_iota(jnp.int32, (64, LANES), 1) < 64
     for group in range(16):
-        rows = dot(order, received[group * 160 : (group + 1) * 160, :])
+        if group % 2 == 0:
+            pair = dot(order, jnp.concatenate([received[(group + i) * 160 : (group + i + 1) * 160, :] for i in range(2)], axis=1))
+        rows = pair[:, :LANES] if group % 2 == 0 else pair[:, LANES:]
         for side in range(2):
             merged = rows[side * 80 : side * 80 + 64]
             exchanged = pltpu.roll(merged, 64, 1)
-            pair = [
+            boxes = [
                 jnp.where(low_lane, merged, exchanged).reshape(GROUP, 1, 16, LANES),
                 jnp.where(low_lane, exchanged, merged).reshape(GROUP, 1, 16, LANES),
             ]
-            points[side, group * LANES : (group + 1) * LANES, :] = jnp.concatenate(pair, axis=1).reshape(LANES, LANES)
+            points[side, group * LANES : (group + 1) * LANES, :] = jnp.concatenate(boxes, axis=1).reshape(LANES, LANES)
             turns[side, group * 8 : (group + 1) * 8, :] = rows[side * 80 + 64 : side * 80 + 72]
             turns[2 + side, group * 8 : (group + 1) * 8, :] = rows[side * 80 + 72 : side * 80 + 80]
     first_half = lax.broadcasted_iota(jnp.int32, (LANES, LANES), 1) < 64
@@ -232,10 +234,9 @@
     for chunk in range(2048 // WHOLE):
         here = pl.ds(chunk * boxes, boxes)
         there = pl.ds(chunk * WHOLE, WHOLE)
-        parts = [halves(per_box(points[side, there, :], turns[side, here, :])) for side in range(2)]
-        both = dot(jnp.concatenate([parts[0][0], parts[1][0]], axis=1), source[...])
+        parts = [per_box(points[side, there, :], turns[side, here, :]).astype(BF16) for side in range(2)]
+        both = dot(jnp.concatenate(parts, axis=1), source[...])
         value = both[:, :LANES] + both[:, LANES:]
-        value = value + dot(jnp.concatenate([parts[0][1], parts[1][1]], axis=1), source[:, :LANES])
         value = rotated(value, turns[2, here, :], turns[3, here, :])
         value = dot_wide(value, wide[2])
         value = rotated(value, factors[0, here, :], factors[1, here, :])
@@ -259,15 +260,16 @@
     out[...] = (own[...] + received[...].astype(F32)).astype(BF16)
 
 
-def call(kernel, outs, args, scratch=(), name=None, spaces=()):
-    whole = pl.BlockSpec(memory_space=pltpu.VMEM)
+def call(kernel, outs, args, scratch=(), name=None, spaces=(), out_spaces=()):
+    out_spaces = list(out_spaces) + [pltpu.VMEM] * (len(outs) - len(out_spaces))
+    targets = [pl.BlockSpec(memory_space=space) for space in out_spaces]
     spaces = list(spaces) + [pltpu.VMEM] * (len(args) - len(spaces))
     shapes = [jax.ShapeDtypeStruct(shape, dtype) for shape, dtype in outs]
     return pl.pallas_call(
         kernel,
         out_shape=shapes if len(shapes) > 1 else shapes[0],
         in_specs=[pl.BlockSpec(memory_space=space) for space in spaces],
-        out_specs=[whole] * len(shapes) if len(shapes) > 1 else whole,
+        out_specs=targets if len(shapes) > 1 else targets[0],
         scratch_shapes=scratch,
         compiler_params=pltpu.CompilerParams(vmem_limit_bytes=32 * 1024 * 1024),
         name=name,

time: 64.4 us -> 63.5 us (0.986)
  Pallas kernels: 8.29 us -> 7.36 us
    pallas_call x5, Pallas kernels: 8.29 us -> 7.36 us  [call(): pl.pallas_call(kernel, out_shape=shapes if len(shapes) > 1 else shapes[0]...]
where the time goes in v6:
time: 63.5 us; the launch traced here: 62.9 us
  waiting for transfers between devices  30 us (47%)
  starting transfers between devices  25.3 us (40%)
  Pallas kernels  7.36 us (12%)
    ppermute x2, waiting for transfers between devices, from_partner(): return lax.ppermute(value, 'narrow', pairs)  20.1 us
    all_to_all x1, starting transfers between devices, body(): lax.all_to_all(packed.reshape(2 * wide, PIECE // 4, 4, LANES), ('wide', '...  15.7 us
    all_to_all x1, waiting for transfers between devices, body(): lax.all_to_all(packed.reshape(2 * wide, PIECE // 4, 4, LANES), ('wide', '...  9.88 us
    ppermute x2, starting transfers between devices, from_partner(): return lax.ppermute(value, 'narrow', pairs)  9.55 us
    pallas_call x5, Pallas kernels, call(): pl.pallas_call(kernel, out_shape=shapes if len(shapes) > 1 else shapes[0]...  7.36 us
  transfers between devices with their start and end apart: 3, of which 3 were waited for; matrix products, arithmetic and copies ran while one was open for 0% of the time, Pallas kernels for 3%

profile of v6, /device:TPU:56, one launch (start us, length us, event | category | flops | bytes accessed | tf_op | source)
XLA Modules:
  0.0 62.9 jit_solution(2931904408087269489)
XLA Ops:
  0.0 2.5 %pack.1 = (bf16[2560,128]{1,0:T(8,128)(2,1)}, f32[112,128]{1,0:T(8,128)S(1)}) custom-call(f32[64,2048]{1,0:T(8,128)} %charges.1, f32[64,128]{1,0:T(8,128)} %leaf_angle.1, f32[2,48,128]{2,1,0:T(8,128)} %level_angle.3, f32[64,128]{1,0:T(8,128)} %out_angle.3), custom_call_target="tpu_custom_call" | custom-call | tf_op jit(solution)/shard_map/pack/pallas_call | solution.py:268
  2.5 0.0 copy-start.7
  2.5 0.0 copy-start.1
  2.5 0.0 copy-start.2
  2.6 0.0 copy-start.3
  2.6 0.0 copy-start.4
  2.6 0.0 copy-start.5
  2.6 0.0 copy-start.6
  2.6 15.7 %all-to-all-start = ((bf16[128,5,4,128]{3,2,1,0:T(4,128)(2,1)}), bf16[128,5,4,128]{3,2,1,0:T(4,128)(2,1)S(1)}, u32[]{:S(2)}, u32[]{:S(2)}) async-start(bf16[128,5,4,128]{3,2,1,0:T(4,128)(2,1)} %bitcast.1), calls=%async_computation | async-start | bytes 1310720 | tf_op jit(solution)/shard_map/all_to_all | solution.py:313
  18.3 0.0 copy-start
  18.4 4.8 %collective-permute-start = (f32[112,128]{1,0:T(8,128)S(1)}, f32[112,128]{1,0:T(8,128)S(1)}, u32[]{:S(2)}, u32[]{:S(2)}) collective-permute-start(f32[112,128]{1,0:T(8,128)S(1)} %get-tuple-element.14), channel_id=1, source_target_pairs={{0,4},{1,5},{2,6},{3,7},{4,0},{5,1},{6,2},{7,3},{8,12},{9,13},{10,... | collective-permute-start | bytes 172040 | tf_op jit(solution)/shard_map/ppermute | solution.py:281
  23.2 0.1 copy.11.evaluate
  23.3 6.4 %collective-permute-done.peer_angle = f32[112,128]{1,0:T(8,128)S(1)} collective-permute-done((f32[112,128]{1,0:T(8,128)S(1)}, f32[112,128]{1,0:T(8,128)S(1)}, u32[]{:S(2)}, u32[]{:S(2)}) %collective-permute-start) | collective-permute-done | bytes 57376 | tf_op jit(solution)/shard_map/ppermute | solution.py:281
  29.7 0.0 copy-done.4
  29.7 0.0 copy-done.5
  29.8 0.0 copy-done.6
  29.8 0.0 copy-done
  29.8 0.6 target.1
  30.3 9.9 %all-to-all-done = bf16[128,5,4,128]{3,2,1,0:T(4,128)(2,1)S(1)} async-done(((bf16[128,5,4,128]{3,2,1,0:T(4,128)(2,1)}), bf16[128,5,4,128]{3,2,1,0:T(4,128)(2,1)S(1)}, u32[]{:S(2)}, u32[]{:S(2)}) %all-to-all-start) | async-done | bytes 655392 | tf_op jit(solution)/shard_map/all_to_all | solution.py:313
  40.2 2.4 %switch.1 = (f32[2048,128]{1,0:T(8,128)S(1)}, bf16[64,2048]{1,0:T(8,128)(2,1)S(1)}) custom-call(s32[1]{0:T(128)} %bitcast.parity, bf16[2560,128]{1,0:T(8,128)(2,1)S(1)} %bitcast.3, bf16[256,256]{1,0:T(8,128)(2,1)S(1)} %get-tuple-element.15.source, bf16[256,128]{1,0:T(8,128)(2,1)S(1)} %get-tuple-element.16.tall, ...), custom_call_target="tpu_custom_call" | custom-call | tf_op jit(solution)/shard_map/switch/pallas_call | solution.py:268
  42.7 4.7 %collective-permute-start.1 = (bf16[64,2048]{1,0:T(8,128)(2,1)S(1)}, bf16[64,2048]{1,0:T(8,128)(2,1)S(1)}, u32[]{:S(2)}, u32[]{:S(2)}) collective-permute-start(bf16[64,2048]{1,0:T(8,128)(2,1)S(1)} %get-tuple-element.20), channel_id=1, source_target_pairs={{0,4},{1,5},{2,6},{3,7},{4,0},{5,1},{6,2},{7,3},{8,12},{9,13},{10,... | collective-permute-start | bytes 786440 | tf_op jit(solution)/shard_map/ppermute | solution.py:281
  47.4 1.1 %last.1.own = f32[64,2048]{1,0:T(8,128)S(1)} custom-call(f32[2048,128]{1,0:T(8,128)S(1)} %get-tuple-element.19.middle, bf16[3,256,256]{2,1,0:T(8,128)(2,1)S(1)} %get-tuple-element.17.wide, f32[8,128,128]{2,1,0:T(8,128)S(1)} %get-tuple-element.18.factors), custom_call_target="tpu_custom_call" | custom-call | tf_op jit(solution)/shard_map/last/pallas_call | solution.py:268
  48.5 13.7 %collective-permute-done.1.received = bf16[64,2048]{1,0:T(8,128)(2,1)S(1)} collective-permute-done((bf16[64,2048]{1,0:T(8,128)(2,1)S(1)}, bf16[64,2048]{1,0:T(8,128)(2,1)S(1)}, u32[]{:S(2)}, u32[]{:S(2)}) %collective-permute-start.1) | collective-permute-done | bytes 262176 | tf_op jit(solution)/shard_map/ppermute | solution.py:281
  62.1 0.8 %add.1 = bf16[64,2048]{1,0:T(8,128)(2,1)} custom-call(f32[64,2048]{1,0:T(8,128)S(1)} %last.1.own, bf16[64,2048]{1,0:T(8,128)(2,1)S(1)} %collective-permute-done.1.received), custom_call_target="tpu_custom_call" | custom-call | tf_op jit(solution)/shard_map/add/pallas_call | solution.py:268
  (4 shorter events, 0.0 us)
Async XLA Ops:
  2.5 20.7 %copy-start.7 = (f32[64,48]{0,1:T(8,128)S(1)}, f32[64,48]{0,1:T(8,128)}, u32[]{:S(2)}) copy-start(f32[64,48]{0,1:T(8,128)} %param.19) | copy-start | bytes 36868
  2.5 27.2 %copy-start.1 = (f32[64,128]{1,0:T(8,128)S(1)}, f32[64,128]{1,0:T(8,128)}, u32[]{:S(2)}) copy-start(f32[64,128]{1,0:T(8,128)} %out_angle.3) | copy-start | bytes 98308
  2.5 27.2 %copy-start.2 = (f32[2,96,96]{2,1,0:T(8,128)S(1)}, f32[2,96,96]{2,1,0:T(8,128)}, u32[]{:S(2)}) copy-start(f32[2,96,96]{2,1,0:T(8,128)} %level_self.1) | copy-start | bytes 221188
  2.6 27.2 %copy-start.3 = (f32[2,96,96]{2,1,0:T(8,128)S(1)}, f32[2,96,96]{2,1,0:T(8,128)}, u32[]{:S(2)}) copy-start(f32[2,96,96]{2,1,0:T(8,128)} %level_peer.1) | copy-start | bytes 221188
  2.6 27.2 %copy-start.4 = (f32[96,96]{1,0:T(8,128)S(1)}, f32[96,96]{1,0:T(8,128)}, u32[]{:S(2)}) copy-start(f32[96,96]{1,0:T(8,128)} %switch_matrix.1) | copy-start | bytes 110596
  2.6 27.2 %copy-start.5 = (f32[48,64]{1,0:T(8,128)S(1)}, f32[48,64]{1,0:T(8,128)}, u32[]{:S(2)}) copy-start(f32[48,64]{1,0:T(8,128)} %lagrange.1) | copy-start | bytes 36868
  2.6 27.2 %copy-start.6 = (f32[48,128]{1,0:T(8,128)S(1)}, f32[48,128]{1,0:T(8,128)}, u32[]{:S(2)}) copy-start(f32[48,128]{1,0:T(8,128)} %switch_angle.1) | copy-start | bytes 73732
  2.6 37.6 %all-to-all-start = ((bf16[128,5,4,128]{3,2,1,0:T(4,128)(2,1)}), bf16[128,5,4,128]{3,2,1,0:T(4,128)(2,1)S(1)}, u32[]{:S(2)}, u32[]{:S(2)}) async-start(bf16[128,5,4,128]{3,2,1,0:T(4,128)(2,1)} %bitcast.1), calls=%async_computation | async-start | bytes 1310720 | tf_op jit(solution)/shard_map/all_to_all | solution.py:313
  18.3 11.4 %copy-start = (f32[2,48,128]{2,1,0:T(8,128)S(1)}, f32[2,48,128]{2,1,0:T(8,128)}, u32[]{:S(2)}) copy-start(f32[2,48,128]{2,1,0:T(8,128)} %level_angle.3) | copy-start | bytes 147460
  18.4 11.4 %collective-permute-start = (f32[112,128]{1,0:T(8,128)S(1)}, f32[112,128]{1,0:T(8,128)S(1)}, u32[]{:S(2)}, u32[]{:S(2)}) collective-permute-start(f32[112,128]{1,0:T(8,128)S(1)} %get-tuple-element.14), channel_id=1, source_target_pairs={{0,4},{1,5},{2,6},{3,7},{4,0},{5,1},{6,2},{7,3},{8,12},{9,13},{10,... | collective-permute-start | bytes 172040 | tf_op jit(solution)/shard_map/ppermute | solution.py:281
  42.7 19.5 %collective-permute-start.1 = (bf16[64,2048]{1,0:T(8,128)(2,1)S(1)}, bf16[64,2048]{1,0:T(8,128)(2,1)S(1)}, u32[]{:S(2)}, u32[]{:S(2)}) collective-permute-start(bf16[64,2048]{1,0:T(8,128)(2,1)S(1)} %get-tuple-element.20), channel_id=1, source_target_pairs={{0,4},{1,5},{2,6},{3,7},{4,0},{5,1},{6,2},{7,3},{8,12},{9,13},{10,... | collective-permute-start | bytes 786440 | tf_op jit(solution)/shard_map/ppermute | solution.py:281

commit v7 on v6

--- a/solution.py
+++ b/solution.py
@@ -131,7 +131,7 @@
     return jnp.concatenate([high, gap, low, gap], axis=0).T
 
 
-def pack_kernel(charges, leaf_angle, level_angle, out_angle, out, far_angle, held, angle, first_angle, sems):
+def pack_kernel(charges, leaf_angle, level_angle, out_angle, out, far_angle, held, angle, first_angle, pieces, sems, sent):
     width = 512
     copies = []
     for step in range(2048 // width):
@@ -153,6 +153,7 @@
         copy.wait()
     leaf_rows = angle_rows(angle[...])
     level_rows = angle_rows(first_angle[...])
+    writes = []
     for pair in range(8):
         rows = []
         for tile in (2 * pair, 2 * pair + 1):
@@ -162,8 +163,14 @@
             boxes = slice(tile * 8, (tile + 1) * 8)
             rows.append(jnp.concatenate([merged, leaf_rows[boxes], level_rows[boxes]], axis=0).astype(BF16))
         rows = dot(order, jnp.concatenate(rows, axis=1)).astype(BF16)
-        out[pair * 320 : pair * 320 + 160, :] = rows[:, :LANES]
-        out[pair * 320 + 160 : pair * 320 + 320, :] = rows[:, LANES:]
+        pieces[pair * 320 : pair * 320 + 160, :] = rows[:, :LANES]
+        pieces[pair * 320 + 160 : pair * 320 + 320, :] = rows[:, LANES:]
+        if pair % 4 == 3:
+            here = pl.ds((pair - 3) * 320, 1280)
+            writes.append(pltpu.make_async_copy(pieces.at[here], out.at[here], sent.at[pair // 4]))
+            writes[-1].start()
+    for copy in writes:
+        copy.wait()
 
 
 def target_kernel(
@@ -304,10 +311,13 @@
             pltpu.VMEM((64, 2048), F32),
             pltpu.VMEM((64, LANES), F32),
             pltpu.VMEM((48, LANES), F32),
+            pltpu.VMEM((128 * PIECE, LANES), BF16),
             pltpu.SemaphoreType.DMA((8,)),
+            pltpu.SemaphoreType.DMA((2,)),
         ],
         name="pack",
         spaces=[pltpu.HBM] * 4,
+        out_spaces=[pltpu.HBM],
     )
     groups = [[w * narrow + r + side for w in range(wide) for side in range(2)] for r in range(0, narrow, 2)]
     packed = lax.all_to_all(

time: 63.5 us -> 63.4 us (level)
  no operation moved by 1% of the time
where the time goes in v7:
time: 63.4 us; the launch traced here: 62.8 us
  waiting for transfers between devices  30 us (47%)
  starting transfers between devices  25.3 us (40%)
  Pallas kernels  7.29 us (11%)
    ppermute x2, waiting for transfers between devices, from_partner(): return lax.ppermute(value, 'narrow', pairs)  20.1 us
    all_to_all x1, starting transfers between devices, body(): lax.all_to_all(packed.reshape(2 * wide, PIECE // 4, 4, LANES), ('wide', '...  15.7 us
    all_to_all x1, waiting for transfers between devices, body(): lax.all_to_all(packed.reshape(2 * wide, PIECE // 4, 4, LANES), ('wide', '...  9.88 us
    ppermute x2, starting transfers between devices, from_partner(): return lax.ppermute(value, 'narrow', pairs)  9.55 us
    pallas_call x5, Pallas kernels, call(): pl.pallas_call(kernel, out_shape=shapes if len(shapes) > 1 else shapes[0]...  7.29 us
  transfers between devices with their start and end apart: 3, of which 3 were waited for; matrix products, arithmetic and copies ran while one was open for 0% of the time, Pallas kernels for 3%

profile of v7, /device:TPU:56, one launch (start us, length us, event | category | flops | bytes accessed | tf_op | source)
XLA Modules:
  0.0 62.8 jit_solution(11245830231570876213)
XLA Ops:
  0.0 2.4 %pack.1 = (bf16[2560,128]{1,0:T(8,128)(2,1)}, f32[112,128]{1,0:T(8,128)S(1)}) custom-call(f32[64,2048]{1,0:T(8,128)} %charges.1, f32[64,128]{1,0:T(8,128)} %leaf_angle.1, f32[2,48,128]{2,1,0:T(8,128)} %level_angle.3, f32[64,128]{1,0:T(8,128)} %out_angle.3), custom_call_target="tpu_custom_call" | custom-call | tf_op jit(solution)/shard_map/pack/pallas_call | solution.py:275
  2.5 0.0 copy-start.7
  2.5 0.0 copy-start.1
  2.5 0.0 copy-start.2
  2.5 0.0 copy-start.3
  2.5 0.0 copy-start.4
  2.5 0.0 copy-start.5
  2.5 0.0 copy-start.6
  2.5 15.7 %all-to-all-start = ((bf16[128,5,4,128]{3,2,1,0:T(4,128)(2,1)}), bf16[128,5,4,128]{3,2,1,0:T(4,128)(2,1)S(1)}, u32[]{:S(2)}, u32[]{:S(2)}) async-start(bf16[128,5,4,128]{3,2,1,0:T(4,128)(2,1)} %bitcast.1), calls=%async_computation | async-start | bytes 1310720 | tf_op jit(solution)/shard_map/all_to_all | solution.py:323
  18.3 0.0 copy-start
  18.3 4.8 %collective-permute-start = (f32[112,128]{1,0:T(8,128)S(1)}, f32[112,128]{1,0:T(8,128)S(1)}, u32[]{:S(2)}, u32[]{:S(2)}) collective-permute-start(f32[112,128]{1,0:T(8,128)S(1)} %get-tuple-element.14), channel_id=1, source_target_pairs={{0,4},{1,5},{2,6},{3,7},{4,0},{5,1},{6,2},{7,3},{8,12},{9,13},{10,... | collective-permute-start | bytes 172040 | tf_op jit(solution)/shard_map/ppermute | solution.py:288
  23.1 0.1 copy.11.evaluate
  23.2 6.4 %collective-permute-done.peer_angle = f32[112,128]{1,0:T(8,128)S(1)} collective-permute-done((f32[112,128]{1,0:T(8,128)S(1)}, f32[112,128]{1,0:T(8,128)S(1)}, u32[]{:S(2)}, u32[]{:S(2)}) %collective-permute-start) | collective-permute-done | bytes 57376 | tf_op jit(solution)/shard_map/ppermute | solution.py:288
  29.7 0.0 copy-done.4
  29.7 0.0 copy-done.5
  29.7 0.0 copy-done.6
  29.7 0.0 copy-done
  29.7 0.6 target.1
  30.3 9.9 %all-to-all-done = bf16[128,5,4,128]{3,2,1,0:T(4,128)(2,1)S(1)} async-done(((bf16[128,5,4,128]{3,2,1,0:T(4,128)(2,1)}), bf16[128,5,4,128]{3,2,1,0:T(4,128)(2,1)S(1)}, u32[]{:S(2)}, u32[]{:S(2)}) %all-to-all-start) | async-done | bytes 655392 | tf_op jit(solution)/shard_map/all_to_all | solution.py:323
  40.2 2.4 %switch.1 = (f32[2048,128]{1,0:T(8,128)S(1)}, bf16[64,2048]{1,0:T(8,128)(2,1)S(1)}) custom-call(s32[1]{0:T(128)} %bitcast.parity, bf16[2560,128]{1,0:T(8,128)(2,1)S(1)} %bitcast.3, bf16[256,256]{1,0:T(8,128)(2,1)S(1)} %get-tuple-element.15.source, bf16[256,128]{1,0:T(8,128)(2,1)S(1)} %get-tuple-element.16.tall, ...), custom_call_target="tpu_custom_call" | custom-call | tf_op jit(solution)/shard_map/switch/pallas_call | solution.py:275
  42.6 4.7 %collective-permute-start.1 = (bf16[64,2048]{1,0:T(8,128)(2,1)S(1)}, bf16[64,2048]{1,0:T(8,128)(2,1)S(1)}, u32[]{:S(2)}, u32[]{:S(2)}) collective-permute-start(bf16[64,2048]{1,0:T(8,128)(2,1)S(1)} %get-tuple-element.20), channel_id=1, source_target_pairs={{0,4},{1,5},{2,6},{3,7},{4,0},{5,1},{6,2},{7,3},{8,12},{9,13},{10,... | collective-permute-start | bytes 786440 | tf_op jit(solution)/shard_map/ppermute | solution.py:288
  47.3 1.1 %last.1.own = f32[64,2048]{1,0:T(8,128)S(1)} custom-call(f32[2048,128]{1,0:T(8,128)S(1)} %get-tuple-element.19.middle, bf16[3,256,256]{2,1,0:T(8,128)(2,1)S(1)} %get-tuple-element.17.wide, f32[8,128,128]{2,1,0:T(8,128)S(1)} %get-tuple-element.18.factors), custom_call_target="tpu_custom_call" | custom-call | tf_op jit(solution)/shard_map/last/pallas_call | solution.py:275
  48.4 13.7 %collective-permute-done.1.received = bf16[64,2048]{1,0:T(8,128)(2,1)S(1)} collective-permute-done((bf16[64,2048]{1,0:T(8,128)(2,1)S(1)}, bf16[64,2048]{1,0:T(8,128)(2,1)S(1)}, u32[]{:S(2)}, u32[]{:S(2)}) %collective-permute-start.1) | collective-permute-done | bytes 262176 | tf_op jit(solution)/shard_map/ppermute | solution.py:288
  62.1 0.8 %add.1 = bf16[64,2048]{1,0:T(8,128)(2,1)} custom-call(f32[64,2048]{1,0:T(8,128)S(1)} %last.1.own, bf16[64,2048]{1,0:T(8,128)(2,1)S(1)} %collective-permute-done.1.received), custom_call_target="tpu_custom_call" | custom-call | tf_op jit(solution)/shard_map/add/pallas_call | solution.py:275
  (4 shorter events, 0.0 us)
Async XLA Ops:
  2.5 20.7 %copy-start.7 = (f32[64,48]{0,1:T(8,128)S(1)}, f32[64,48]{0,1:T(8,128)}, u32[]{:S(2)}) copy-start(f32[64,48]{0,1:T(8,128)} %param.19) | copy-start | bytes 36868
  2.5 27.2 %copy-start.1 = (f32[64,128]{1,0:T(8,128)S(1)}, f32[64,128]{1,0:T(8,128)}, u32[]{:S(2)}) copy-start(f32[64,128]{1,0:T(8,128)} %out_angle.3) | copy-start | bytes 98308
  2.5 27.2 %copy-start.2 = (f32[2,96,96]{2,1,0:T(8,128)S(1)}, f32[2,96,96]{2,1,0:T(8,128)}, u32[]{:S(2)}) copy-start(f32[2,96,96]{2,1,0:T(8,128)} %level_self.1) | copy-start | bytes 221188
  2.5 27.2 %copy-start.3 = (f32[2,96,96]{2,1,0:T(8,128)S(1)}, f32[2,96,96]{2,1,0:T(8,128)}, u32[]{:S(2)}) copy-start(f32[2,96,96]{2,1,0:T(8,128)} %level_peer.1) | copy-start | bytes 221188
  2.5 27.2 %copy-start.4 = (f32[96,96]{1,0:T(8,128)S(1)}, f32[96,96]{1,0:T(8,128)}, u32[]{:S(2)}) copy-start(f32[96,96]{1,0:T(8,128)} %switch_matrix.1) | copy-start | bytes 110596
  2.5 27.2 %copy-start.5 = (f32[48,64]{1,0:T(8,128)S(1)}, f32[48,64]{1,0:T(8,128)}, u32[]{:S(2)}) copy-start(f32[48,64]{1,0:T(8,128)} %lagrange.1) | copy-start | bytes 36868
  2.5 27.2 %copy-start.6 = (f32[48,128]{1,0:T(8,128)S(1)}, f32[48,128]{1,0:T(8,128)}, u32[]{:S(2)}) copy-start(f32[48,128]{1,0:T(8,128)} %switch_angle.1) | copy-start | bytes 73732
  2.5 37.6 %all-to-all-start = ((bf16[128,5,4,128]{3,2,1,0:T(4,128)(2,1)}), bf16[128,5,4,128]{3,2,1,0:T(4,128)(2,1)S(1)}, u32[]{:S(2)}, u32[]{:S(2)}) async-start(bf16[128,5,4,128]{3,2,1,0:T(4,128)(2,1)} %bitcast.1), calls=%async_computation | async-start | bytes 1310720 | tf_op jit(solution)/shard_map/all_to_all | solution.py:323
  18.3 11.4 %copy-start = (f32[2,48,128]{2,1,0:T(8,128)S(1)}, f32[2,48,128]{2,1,0:T(8,128)}, u32[]{:S(2)}) copy-start(f32[2,48,128]{2,1,0:T(8,128)} %level_angle.3) | copy-start | bytes 147460
  18.3 11.4 %collective-permute-start = (f32[112,128]{1,0:T(8,128)S(1)}, f32[112,128]{1,0:T(8,128)S(1)}, u32[]{:S(2)}, u32[]{:S(2)}) collective-permute-start(f32[112,128]{1,0:T(8,128)S(1)} %get-tuple-element.14), channel_id=1, source_target_pairs={{0,4},{1,5},{2,6},{3,7},{4,0},{5,1},{6,2},{7,3},{8,12},{9,13},{10,... | collective-permute-start | bytes 172040 | tf_op jit(solution)/shard_map/ppermute | solution.py:288
  42.6 19.5 %collective-permute-start.1 = (bf16[64,2048]{1,0:T(8,128)(2,1)S(1)}, bf16[64,2048]{1,0:T(8,128)(2,1)S(1)}, u32[]{:S(2)}, u32[]{:S(2)}) collective-permute-start(bf16[64,2048]{1,0:T(8,128)(2,1)S(1)} %get-tuple-element.20), channel_id=1, source_target_pairs={{0,4},{1,5},{2,6},{3,7},{4,0},{5,1},{6,2},{7,3},{8,12},{9,13},{10,... | collective-permute-start | bytes 786440 | tf_op jit(solution)/shard_map/ppermute | solution.py:288

commit v8 on v7

--- a/solution.py
+++ b/solution.py
@@ -149,12 +149,15 @@
         copy.start()
     order = piece_rows(False)
     low_lane = lax.broadcasted_iota(jnp.int32, (64, LANES), 1) < 64
-    for copy in near + copies + far:
+    for copy in near:
         copy.wait()
     leaf_rows = angle_rows(angle[...])
     level_rows = angle_rows(first_angle[...])
     writes = []
     for pair in range(8):
+        if pair % 4 == 0:
+            for copy in copies[pair // 2 : pair // 2 + 2]:
+                copy.wait()
         rows = []
         for tile in (2 * pair, 2 * pair + 1):
             points = held[:, tile * LANES : (tile + 1) * LANES]
@@ -169,7 +172,7 @@
             here = pl.ds((pair - 3) * 320, 1280)
             writes.append(pltpu.make_async_copy(pieces.at[here], out.at[here], sent.at[pair // 4]))
             writes[-1].start()
-    for copy in writes:
+    for copy in writes + far:
         copy.wait()
 
 

time: 63.4 us -> 63.5 us (level)
  no operation moved by 1% of the time
where the time goes in v8:
time: 63.5 us; the launch traced here: 62.9 us
  waiting for transfers between devices  30 us (47%)
  starting transfers between devices  25.3 us (40%)
  Pallas kernels  7.3 us (11%)
    ppermute x2, waiting for transfers between devices, from_partner(): return lax.ppermute(value, 'narrow', pairs)  20.1 us
    all_to_all x1, starting transfers between devices, body(): lax.all_to_all(packed.reshape(2 * wide, PIECE // 4, 4, LANES), ('wide', '...  15.7 us
    all_to_all x1, waiting for transfers between devices, body(): lax.all_to_all(packed.reshape(2 * wide, PIECE // 4, 4, LANES), ('wide', '...  9.88 us
    ppermute x2, starting transfers between devices, from_partner(): return lax.ppermute(value, 'narrow', pairs)  9.56 us
    pallas_call x5, Pallas kernels, call(): pl.pallas_call(kernel, out_shape=shapes if len(shapes) > 1 else shapes[0]...  7.3 us
  transfers between devices with their start and end apart: 3, of which 3 were waited for; matrix products, arithmetic and copies ran while one was open for 0% of the time, Pallas kernels for 3%

profile of v8, /device:TPU:56, one launch (start us, length us, event | category | flops | bytes accessed | tf_op | source)
XLA Modules:
  0.0 62.9 jit_solution(15710867679531152081)
XLA Ops:
  0.0 2.5 %pack.1 = (bf16[2560,128]{1,0:T(8,128)(2,1)}, f32[112,128]{1,0:T(8,128)S(1)}) custom-call(f32[64,2048]{1,0:T(8,128)} %charges.1, f32[64,128]{1,0:T(8,128)} %leaf_angle.1, f32[2,48,128]{2,1,0:T(8,128)} %level_angle.3, f32[64,128]{1,0:T(8,128)} %out_angle.3), custom_call_target="tpu_custom_call" | custom-call | tf_op jit(solution)/shard_map/pack/pallas_call | solution.py:278
  2.5 0.0 copy-start.7
  2.5 0.0 copy-start.1
  2.5 0.0 copy-start.2
  2.5 0.0 copy-start.3
  2.5 0.0 copy-start.4
  2.5 0.0 copy-start.5
  2.5 0.0 copy-start.6
  2.6 15.7 %all-to-all-start = ((bf16[128,5,4,128]{3,2,1,0:T(4,128)(2,1)}), bf16[128,5,4,128]{3,2,1,0:T(4,128)(2,1)S(1)}, u32[]{:S(2)}, u32[]{:S(2)}) async-start(bf16[128,5,4,128]{3,2,1,0:T(4,128)(2,1)} %bitcast.1), calls=%async_computation | async-start | bytes 1310720 | tf_op jit(solution)/shard_map/all_to_all | solution.py:326
  18.3 0.0 copy-start
  18.3 4.8 %collective-permute-start = (f32[112,128]{1,0:T(8,128)S(1)}, f32[112,128]{1,0:T(8,128)S(1)}, u32[]{:S(2)}, u32[]{:S(2)}) collective-permute-start(f32[112,128]{1,0:T(8,128)S(1)} %get-tuple-element.14), channel_id=1, source_target_pairs={{0,4},{1,5},{2,6},{3,7},{4,0},{5,1},{6,2},{7,3},{8,12},{9,13},{10,... | collective-permute-start | bytes 172040 | tf_op jit(solution)/shard_map/ppermute | solution.py:291
  23.2 0.0 copy-done.7
  23.2 0.1 copy.11.evaluate
  23.2 6.4 %collective-permute-done.peer_angle = f32[112,128]{1,0:T(8,128)S(1)} collective-permute-done((f32[112,128]{1,0:T(8,128)S(1)}, f32[112,128]{1,0:T(8,128)S(1)}, u32[]{:S(2)}, u32[]{:S(2)}) %collective-permute-start) | collective-permute-done | bytes 57376 | tf_op jit(solution)/shard_map/ppermute | solution.py:291
  29.7 0.0 copy-done.1
  29.7 0.0 copy-done.2
  29.7 0.0 copy-done.3
  29.7 0.6 target.1
  30.3 9.9 %all-to-all-done = bf16[128,5,4,128]{3,2,1,0:T(4,128)(2,1)S(1)} async-done(((bf16[128,5,4,128]{3,2,1,0:T(4,128)(2,1)}), bf16[128,5,4,128]{3,2,1,0:T(4,128)(2,1)S(1)}, u32[]{:S(2)}, u32[]{:S(2)}) %all-to-all-start) | async-done | bytes 655392 | tf_op jit(solution)/shard_map/all_to_all | solution.py:326
  40.2 2.4 %switch.1 = (f32[2048,128]{1,0:T(8,128)S(1)}, bf16[64,2048]{1,0:T(8,128)(2,1)S(1)}) custom-call(s32[1]{0:T(128)} %bitcast.parity, bf16[2560,128]{1,0:T(8,128)(2,1)S(1)} %bitcast.3, bf16[256,256]{1,0:T(8,128)(2,1)S(1)} %get-tuple-element.15.source, bf16[256,128]{1,0:T(8,128)(2,1)S(1)} %get-tuple-element.16.tall, ...), custom_call_target="tpu_custom_call" | custom-call | tf_op jit(solution)/shard_map/switch/pallas_call | solution.py:278
  42.6 4.7 %collective-permute-start.1 = (bf16[64,2048]{1,0:T(8,128)(2,1)S(1)}, bf16[64,2048]{1,0:T(8,128)(2,1)S(1)}, u32[]{:S(2)}, u32[]{:S(2)}) collective-permute-start(bf16[64,2048]{1,0:T(8,128)(2,1)S(1)} %get-tuple-element.20), channel_id=1, source_target_pairs={{0,4},{1,5},{2,6},{3,7},{4,0},{5,1},{6,2},{7,3},{8,12},{9,13},{10,... | collective-permute-start | bytes 786440 | tf_op jit(solution)/shard_map/ppermute | solution.py:291
  47.3 1.1 %last.1.own = f32[64,2048]{1,0:T(8,128)S(1)} custom-call(f32[2048,128]{1,0:T(8,128)S(1)} %get-tuple-element.19.middle, bf16[3,256,256]{2,1,0:T(8,128)(2,1)S(1)} %get-tuple-element.17.wide, f32[8,128,128]{2,1,0:T(8,128)S(1)} %get-tuple-element.18.factors), custom_call_target="tpu_custom_call" | custom-call | tf_op jit(solution)/shard_map/last/pallas_call | solution.py:278
  48.4 13.7 %collective-permute-done.1.received = bf16[64,2048]{1,0:T(8,128)(2,1)S(1)} collective-permute-done((bf16[64,2048]{1,0:T(8,128)(2,1)S(1)}, bf16[64,2048]{1,0:T(8,128)(2,1)S(1)}, u32[]{:S(2)}, u32[]{:S(2)}) %collective-permute-start.1) | collective-permute-done | bytes 262176 | tf_op jit(solution)/shard_map/ppermute | solution.py:291
  62.1 0.8 %add.1 = bf16[64,2048]{1,0:T(8,128)(2,1)} custom-call(f32[64,2048]{1,0:T(8,128)S(1)} %last.1.own, bf16[64,2048]{1,0:T(8,128)(2,1)S(1)} %collective-permute-done.1.received), custom_call_target="tpu_custom_call" | custom-call | tf_op jit(solution)/shard_map/add/pallas_call | solution.py:278
  (4 shorter events, 0.0 us)
Async XLA Ops:
  2.5 20.7 %copy-start.7 = (f32[64,48]{0,1:T(8,128)S(1)}, f32[64,48]{0,1:T(8,128)}, u32[]{:S(2)}) copy-start(f32[64,48]{0,1:T(8,128)} %param.19) | copy-start | bytes 36868
  2.5 27.2 %copy-start.1 = (f32[64,128]{1,0:T(8,128)S(1)}, f32[64,128]{1,0:T(8,128)}, u32[]{:S(2)}) copy-start(f32[64,128]{1,0:T(8,128)} %out_angle.3) | copy-start | bytes 98308
  2.5 27.2 %copy-start.2 = (f32[2,96,96]{2,1,0:T(8,128)S(1)}, f32[2,96,96]{2,1,0:T(8,128)}, u32[]{:S(2)}) copy-start(f32[2,96,96]{2,1,0:T(8,128)} %level_self.1) | copy-start | bytes 221188
  2.5 27.2 %copy-start.3 = (f32[2,96,96]{2,1,0:T(8,128)S(1)}, f32[2,96,96]{2,1,0:T(8,128)}, u32[]{:S(2)}) copy-start(f32[2,96,96]{2,1,0:T(8,128)} %level_peer.1) | copy-start | bytes 221188
  2.5 27.2 %copy-start.4 = (f32[96,96]{1,0:T(8,128)S(1)}, f32[96,96]{1,0:T(8,128)}, u32[]{:S(2)}) copy-start(f32[96,96]{1,0:T(8,128)} %switch_matrix.1) | copy-start | bytes 110596
  2.5 27.2 %copy-start.5 = (f32[48,64]{1,0:T(8,128)S(1)}, f32[48,64]{1,0:T(8,128)}, u32[]{:S(2)}) copy-start(f32[48,64]{1,0:T(8,128)} %lagrange.1) | copy-start | bytes 36868
  2.5 27.2 %copy-start.6 = (f32[48,128]{1,0:T(8,128)S(1)}, f32[48,128]{1,0:T(8,128)}, u32[]{:S(2)}) copy-start(f32[48,128]{1,0:T(8,128)} %switch_angle.1) | copy-start | bytes 73732
  2.6 37.6 %all-to-all-start = ((bf16[128,5,4,128]{3,2,1,0:T(4,128)(2,1)}), bf16[128,5,4,128]{3,2,1,0:T(4,128)(2,1)S(1)}, u32[]{:S(2)}, u32[]{:S(2)}) async-start(bf16[128,5,4,128]{3,2,1,0:T(4,128)(2,1)} %bitcast.1), calls=%async_computation | async-start | bytes 1310720 | tf_op jit(solution)/shard_map/all_to_all | solution.py:326
  18.3 11.4 %copy-start = (f32[2,48,128]{2,1,0:T(8,128)S(1)}, f32[2,48,128]{2,1,0:T(8,128)}, u32[]{:S(2)}) copy-start(f32[2,48,128]{2,1,0:T(8,128)} %level_angle.3) | copy-start | bytes 147460
  18.3 11.4 %collective-permute-start = (f32[112,128]{1,0:T(8,128)S(1)}, f32[112,128]{1,0:T(8,128)S(1)}, u32[]{:S(2)}, u32[]{:S(2)}) collective-permute-start(f32[112,128]{1,0:T(8,128)S(1)} %get-tuple-element.14), channel_id=1, source_target_pairs={{0,4},{1,5},{2,6},{3,7},{4,0},{5,1},{6,2},{7,3},{8,12},{9,13},{10,... | collective-permute-start | bytes 172040 | tf_op jit(solution)/shard_map/ppermute | solution.py:291
  42.6 19.5 %collective-permute-start.1 = (bf16[64,2048]{1,0:T(8,128)(2,1)S(1)}, bf16[64,2048]{1,0:T(8,128)(2,1)S(1)}, u32[]{:S(2)}, u32[]{:S(2)}) collective-permute-start(bf16[64,2048]{1,0:T(8,128)(2,1)S(1)} %get-tuple-element.20), channel_id=1, source_target_pairs={{0,4},{1,5},{2,6},{3,7},{4,0},{5,1},{6,2},{7,3},{8,12},{9,13},{10,... | collective-permute-start | bytes 786440 | tf_op jit(solution)/shard_map/ppermute | solution.py:291
